TPU v7x, 256 devices: a whole 4x4x8 slice. The times are simulated.
256 devices in a mesh: group: 8 (over x, core), member: 32 (over y, z).
Axes of the slice: x: 4, y: 4, z: 8, core: 2. Of those that a mesh axis runs over, the one named last changes fastest.
Arguments:
- q_rows: bfloat16 [65536, 8192], P(('group', 'member')), may hold values from -36 to 36
- own_kv: bfloat16 [65536, 1024], P(('group', 'member')), may hold values from -6 to 6
- cache: bfloat16 [1024, 64, 1024], P(('group', 'member')), may hold values from -6 to 6
- recomp_hidden: bfloat16 [512, 8, 16, 4096], P(('group', 'member')), may hold values from -6 to 6
- w_kv: bfloat16 [4096, 1024], P('member', 'group'), may hold values from -0.09375 to 0.09375
- retrieval: int32 [512, 8], P(('group', 'member')), may hold values from 0 to 127, as said below
- positions: int32 [512, 8, 16], P(('group', 'member')), may hold values from 0 to 63, as said below
Outputs:
- attn_out: bfloat16 [65536, 8192], P(('group', 'member'))
Inputs may be any that keep to these rules, and one draw needn't show every extreme that they name: `retrieval`: the 8 passages of one query are different. Passage i of a group's corpus is held by the device of member index i // 4 in that group. The queries of one device name at most 1 passages held by any one device, and this bound is reached. The 16 positions of one retrieved passage are different.
All inputs are finite; a program needn't handle non-finite values.
Results may differ from a plain program's by a relative error of at most 0.0054.
Values may be sent and summed in bfloat16 or wider, within the bound.
A program may use at most 128 MiB of HBM per device.

v0:
```python
import jax
import jax.numpy as jnp
from jax import lax
from jax.sharding import PartitionSpec as P

D = 4096
HQ = 64
KVH = 4
HD = 128
TOPP = 8
QLEN = 128
PLEN = 64
RECOMP = 16


EPSILON = 1e-06


def local(q_rows, own_kv, cache, recomp_hidden, w_kv, retrieval, positions):
    query_count = retrieval.shape[0]
    requests = query_count * TOPP
    kv_width = 2 * KVH * HD
    grouped = HQ // KVH
    span_keys = TOPP * PLEN + QLEN
    scale = 1.0 / HD**0.5
    row_count = requests * RECOMP
    hidden = recomp_hidden.reshape(row_count, D).astype(jnp.float32)
    normed = (
        hidden * lax.rsqrt(jnp.mean(hidden * hidden, axis=1, keepdims=True) + EPSILON)
    ).astype(jnp.bfloat16)
    head_columns = lax.all_gather(w_kv, "group", axis=1, tiled=True)
    projected = jnp.dot(
        normed,
        lax.all_gather(head_columns, "member", axis=0, tiled=True),
        preferred_element_type=jnp.float32,
    )
    recomputed = projected.astype(jnp.bfloat16).reshape(requests, RECOMP, kv_width)
    wanted = retrieval.reshape(requests)
    pass_local = cache.shape[0]
    holders_count = lax.axis_size("member")
    my_index = lax.axis_index("member")
    capacity = -(-requests // holders_count)
    request_table = lax.all_gather(wanted.reshape(1, requests), "member", axis=0, tiled=True)
    mine_mask = request_table // pass_local == my_index
    earlier_mask = (jnp.arange(requests)[:, None] < jnp.arange(requests)[None, :]).astype(jnp.int32)
    slot_rank = jnp.dot(mine_mask.astype(jnp.int32), earlier_mask)
    slot_table = mine_mask[:, None, :] & (
        slot_rank[:, None, :] == jnp.arange(capacity)[None, :, None]
    )
    local_index = jnp.sum(
        jnp.where(slot_table, (request_table % pass_local)[:, None, :], 0), axis=2
    )
    slot_filled = jnp.any(slot_table, axis=2)
    outgoing = jnp.where(
        slot_filled[:, :, None, None], cache[local_index], jnp.zeros((), cache.dtype)
    )
    arrived = lax.all_to_all(outgoing, "member", split_axis=0, concat_axis=0, tiled=True)
    holder_of = wanted // pass_local
    same_holder = holder_of[:, None] == holder_of[None, :]
    before_me = jnp.arange(requests)[None, :] < jnp.arange(requests)[:, None]
    copy_rank = jnp.sum((same_holder & before_me).astype(jnp.int32), axis=1)
    blocks = arrived.reshape(holders_count * capacity, PLEN, kv_width)[
        holder_of * capacity + copy_rank
    ]
    spots = positions.reshape(requests, RECOMP)
    onehot = spots[:, :, None] == jnp.arange(PLEN)[None, None, :]
    covered = jnp.any(onehot, axis=1)
    placed = jnp.einsum(
        "krp,kre->kpe", onehot.astype(jnp.bfloat16), recomputed, preferred_element_type=jnp.float32
    ).astype(jnp.bfloat16)
    context = jnp.where(covered[:, :, None], placed, blocks).reshape(
        query_count, TOPP * PLEN, kv_width
    )
    context = jnp.concatenate([context, own_kv.reshape(query_count, QLEN, kv_width)], axis=1)
    keys = context[:, :, : KVH * HD].reshape(query_count, span_keys, KVH, HD)
    values = context[:, :, KVH * HD :].reshape(query_count, span_keys, KVH, HD)
    queries = q_rows.reshape(query_count, QLEN, KVH, grouped, HD)
    token_pos = jnp.arange(QLEN)[:, None]
    key_pos = jnp.arange(span_keys)[None, :]
    visible = (key_pos < TOPP * PLEN) | (key_pos - TOPP * PLEN <= token_pos)

    def attend(operands):
        query_block, key_block, value_block = operands
        scores = (
            jnp.einsum("tkgd,skd->kgts", query_block, key_block, preferred_element_type=jnp.float32)
            * scale
        )
        scores = jnp.where(visible, scores, -jnp.inf)
        peak = jnp.max(scores, axis=-1, keepdims=True)
        expd = jnp.exp(scores - peak)
        probs = (expd / jnp.sum(expd, axis=-1, keepdims=True)).astype(jnp.bfloat16)
        output = jnp.einsum(
            "kgts,skd->tkgd", probs, value_block, preferred_element_type=jnp.float32
        )
        return output.astype(jnp.bfloat16).reshape(QLEN, HQ * HD)

    results = lax.map(attend, (queries, keys, values))
    return results.reshape(query_count * QLEN, HQ * HD)


def solution(mesh):
    placed = (
        P(("group", "member"), None),
        P(("group", "member"), None),
        P(("group", "member"), None, None),
        P(("group", "member"), None, None, None),
        P("member", "group"),
        P(("group", "member"), None),
        P(("group", "member"), None, None),
    )
    return jax.shard_map(
        local, mesh=mesh, in_specs=placed, out_specs=P(("group", "member"), None), check_vma=False
    )
```

profile of v0, /device:TPU:8, one launch (start us, length us, event | category | flops | bytes accessed | tf_op | source)
XLA Modules:
  0.0 286.1 jit_solution(2852515802772880683)
XLA Ops:
  6.5 13.6 %all_gather.9 = bf16[128,1024]{1,0:T(8,128)(2,1)} all-gather(bf16[128,128]{1,0:T(8,128)(2,1)} %param.13), channel_id=1, replica_groups=mesh['group'=8,'member'=32] {'group'}, dimensions={1}, use_global_device_ids=true | all-gather | bytes 294912 | tf_op jit(solution)/shard_map/all_gather | solution.py:31
  20.2 0.8 reshape.252
  21.0 41.5 %all-gather = s32[32,1,16]{2,1,0:T(1,128)S(1)} all-gather(s32[1,1,16]{2,1,0:T(1,128)S(1)} %reshape.252), channel_id=1, replica_groups=mesh['group'=8,'member'=32] {'member'}, dimensions={0}, use_global_device_ids=true | all-gather | bytes 2112 | tf_op jit(solution)/shard_map/all_gather | solution.py:43
  62.5 0.2 fusion.37
  62.8 2.8 gather_fusion
  65.6 4.5 %bitcast_select_fusion.4 = bf16[32,1,64,1024]{3,2,1,0:T(8,128)(2,1)} fusion(bf16[32,64,1024]{2,1,0:T(8,128)(2,1)} %gather_fusion, pred[32]{0:T(512)(128)(4,1)S(1)} %reduce_or.19), kind=kLoop, calls=%fused_computation.31 | loop fusion | flops 2097152 | bytes 8388640 | tf_op jit(solution)/shard_map/jit(_where)/select_n | solution.py:54
  70.1 7.2 %all-to-all-start = ((bf16[32,1,64,1024]{3,2,1,0:T(8,128)(2,1)}), bf16[32,1,64,1024]{3,2,1,0:T(8,128)(2,1)}, u32[]{:S(2)}, u32[]{:S(2)}) async-start(bf16[32,1,64,1024]{3,2,1,0:T(8,128)(2,1)} %bitcast_select_fusion.4), calls=%async_computation | async-start | bytes 8388608 | tf_op jit(solution)/shard_map/all_to_all | solution.py:57
  77.5 0.5 multiply_reduce_fusion
  78.1 0.3 copy.35
  78.4 5.4 %copy.46 = bf16[32,8,64,128]{3,2,1,0:T(8,128)(2,1)} copy(bf16[32,8,64,128]{3,1,2,0:T(8,128)(2,1)} %bitcast.134) | data formatting | bytes 8388608
  83.8 0.2 convert_reduce_fusion
  84.1 1.9 fusion.30
  86.1 116.4 %all-to-all-done = bf16[32,1,64,1024]{3,2,1,0:T(8,128)(2,1)} async-done(((bf16[32,1,64,1024]{3,2,1,0:T(8,128)(2,1)}), bf16[32,1,64,1024]{3,2,1,0:T(8,128)(2,1)}, u32[]{:S(2)}, u32[]{:S(2)}) %all-to-all-start) | async-done | bytes 4194336 | tf_op jit(solution)/shard_map/all_to_all | solution.py:57
  202.5 2.9 %gather_fusion.1 = bf16[16,64,1024]{2,1,0:T(8,128)(2,1)S(1)} fusion(bf16[32,64,1024]{2,1,0:T(8,128)(2,1)} %bitcast.7, s32[1024]{0:T(1024)S(1)} %pad_clamp_fusion), kind=kCustom, calls=%fused_computation.1 | custom fusion | bytes 4194368 | tf_op jit(solution)/shard_map/gather | solution.py:62
  205.4 6.3 %convolution_convert_fusion = bf16[256,1024]{1,0:T(8,128)(2,1)S(1)} fusion(bf16[256,4096]{1,0:T(8,128)(2,1)} %fusion.30, bf16[4096,1024]{1,0:T(8,128)(2,1)} %all-gather.3.cloned.1.call-done), kind=kOutput, calls=%fused_computation.40 | convolution fusion | flops 2147745792 | bytes 11010048 | tf_op jit(solution)/shard_map/dot_general | solution.py:32
  211.8 2.6 convert_select_fusion
  214.4 2.9 copy.34
  217.2 1.7 pad_maximum_fusion
  219.0 59.2 %while.11 = (s32[]{:T(128)}, bf16[2,128,8192]{2,1,0:T(8,128)(2,1)}, bf16[2,640,4,128]{1,3,2,0:T(8,128)(2,1)}, bf16[2,640,4,128]{1,3,2,0:T(8,128)(2,1)}, bf16[2,1...) while((s32[]{:T(128)}, bf16[2,128,8192]{2,1,0:T(8,128)(2,1)}, ...), condition=%wide.region_8.9_spmd.clone, body=%wide.region_5.8_spmd.clone.sunk | while | flops 2717024768 | bytes 60265176 | solution.py:97
  219.0 2.0 constant_dynamic-slice_fusion.2
  221.0 0.2 fusion.72
  221.2 12.5 %fusion.73 = (f32[4,16,128]{2,1,0:T(8,128)S(1)}, f32[4,16,128,640]{2,3,1,0:T(8,128)}) fusion(pred[128,640]{0,1:T(8,128)(4,1)S(1)} %fusion.72, bf16[1,128,4,16,128]{4,3,2,1,0:T(8,128)(2,1)S(1)} %constant_dynamic-slice_fusion.2, bf16[2,640,4,128]{1,3,2,0:T(8,128)(2,1)} %get-tuple-element.170, s32[]{:T(128)} %get-tuple-element.159), kind=kOutput, calls=%fused_computation.92.clone.1 | convolution fusion | flops 1363149440 | bytes 23839232 | tf_op jit(solution)/shard_map/while/body/eval_jaxpr/sub | solution.py:90
  233.8 10.4 %fusion.74 = bf16[4,128,16,128]{3,1,2,0:T(8,128)(2,1)} fusion(f32[4,16,128,640]{2,3,1,0:T(8,128)} %get-tuple-element.149, f32[4,16,128]{2,1,0:T(8,128)S(1)} %get-tuple-element.150, bf16[2,640,4,128]{1,3,2,0:T(8,128)(2,1)} %get-tuple-element.169, s32[]{:T(128)} %get-tuple-element.159), kind=kOutput, calls=%fused_computation.14.clone.1 | convolution fusion | flops 1353711616 | bytes 23757312 | tf_op jit(solution)/shard_map/while/body/eval_jaxpr/kgts,skd->tkgd/dot_general | solution.py:92
  244.2 2.9 %copy.61 = bf16[1,128,8192]{2,1,0:T(8,128)(2,1)S(1)} copy(bf16[1,128,8192]{1,2,0:T(8,128)(2,1)} %bitcast.131) | data formatting | bytes 4194304 | tf_op jit(solution)/shard_map/while/body/jit(dynamic_update_index_in_dim)/dynamic_update_slice | solution.py:97
  247.1 1.5 constant_dynamic-update-slice_fusion.2
  248.6 2.0 constant_dynamic-slice_fusion.2
  250.6 0.2 fusion.72
  250.8 12.5 %fusion.73 = (f32[4,16,128]{2,1,0:T(8,128)S(1)}, f32[4,16,128,640]{2,3,1,0:T(8,128)}) fusion(pred[128,640]{0,1:T(8,128)(4,1)S(1)} %fusion.72, bf16[1,128,4,16,128]{4,3,2,1,0:T(8,128)(2,1)S(1)} %constant_dynamic-slice_fusion.2, bf16[2,640,4,128]{1,3,2,0:T(8,128)(2,1)} %get-tuple-element.170, s32[]{:T(128)} %get-tuple-element.159), kind=kOutput, calls=%fused_computation.92.clone.1 | convolution fusion | flops 1363149440 | bytes 23839232 | tf_op jit(solution)/shard_map/while/body/eval_jaxpr/sub | solution.py:90
  263.4 10.4 %fusion.74 = bf16[4,128,16,128]{3,1,2,0:T(8,128)(2,1)} fusion(f32[4,16,128,640]{2,3,1,0:T(8,128)} %get-tuple-element.149, f32[4,16,128]{2,1,0:T(8,128)S(1)} %get-tuple-element.150, bf16[2,640,4,128]{1,3,2,0:T(8,128)(2,1)} %get-tuple-element.169, s32[]{:T(128)} %get-tuple-element.159), kind=kOutput, calls=%fused_computation.14.clone.1 | convolution fusion | flops 1353711616 | bytes 23757312 | tf_op jit(solution)/shard_map/while/body/eval_jaxpr/kgts,skd->tkgd/dot_general | solution.py:92
  273.8 2.9 %copy.61 = bf16[1,128,8192]{2,1,0:T(8,128)(2,1)S(1)} copy(bf16[1,128,8192]{1,2,0:T(8,128)(2,1)} %bitcast.131) | data formatting | bytes 4194304 | tf_op jit(solution)/shard_map/while/body/jit(dynamic_update_index_in_dim)/dynamic_update_slice | solution.py:97
  276.7 1.5 constant_dynamic-update-slice_fusion.2
  278.2 1.0 copy-done.1
  (29 shorter events, 0.6 us)
Async XLA Ops:
  6.5 56.2 %copy-start = (bf16[4,64,1024]{2,1,0:T(8,128)(2,1)S(1)}, bf16[4,64,1024]{2,1,0:T(8,128)(2,1)}, u32[]{:S(2)}) copy-start(bf16[4,64,1024]{2,1,0:T(8,128)(2,1)} %param.11) | copy-start | bytes 1572868
  6.5 198.9 %all-gather.3.cloned.1.call-start = ((), (), s32[]{:S(2)}) async-start(), calls=%async_computation.1 | async-start | bytes 8650752 | tf_op jit(solution)/shard_map/all_gather | solution.py:34
  70.1 7.2 %copy-start.5 = (s32[2,8]{1,0:T(2,128)S(1)}, s32[2,8]{1,0:T(2,128)}, u32[]{:S(2)}) copy-start(s32[2,8]{1,0:T(2,128)} %param.14) | copy-start | bytes 196
  70.1 7.4 %copy-start.2 = (bf16[2,8,16,4096]{3,2,1,0:T(8,128)(2,1)S(1)}, bf16[2,8,16,4096]{3,2,1,0:T(8,128)(2,1)}, u32[]{:S(2)}) copy-start(bf16[2,8,16,4096]{3,2,1,0:T(8,128)(2,1)} %param.12) | copy-start | bytes 6291460
  70.1 8.0 %copy-start.3 = (bf16[256,1024]{1,0:T(8,128)(2,1)S(1)}, bf16[256,1024]{1,0:T(8,128)(2,1)}, u32[]{:S(2)}) copy-start(bf16[256,1024]{1,0:T(8,128)(2,1)} %param.10) | copy-start | bytes 1572868
  70.1 132.4 %all-to-all-start = ((bf16[32,1,64,1024]{3,2,1,0:T(8,128)(2,1)}), bf16[32,1,64,1024]{3,2,1,0:T(8,128)(2,1)}, u32[]{:S(2)}, u32[]{:S(2)}) async-start(bf16[32,1,64,1024]{3,2,1,0:T(8,128)(2,1)} %bitcast_select_fusion.4), calls=%async_computation | async-start | bytes 8388608 | tf_op jit(solution)/shard_map/all_to_all | solution.py:57
  78.4 5.6 %copy-start.4 = (s32[2,8,16]{2,1,0:T(8,128)S(1)}, s32[2,8,16]{2,1,0:T(8,128)}, u32[]{:S(2)}) copy-start(s32[2,8,16]{2,1,0:T(8,128)} %param.15) | copy-start | bytes 3076
  278.2 1.0 copy-start.1
Sparse Core Ops, SparseCore 0:
  20.3 182.9 all-gather.2
where the time goes:
time: 288 us; the launch traced here: 286 us
  waiting for transfers between devices  116 us (40%)
  blocking collectives  55.1 us (19%)
  matrix products  55.1 us (19%)
  local copies, waits for them, and re-layouts  29.1 us (10%)
  between operations  13.5 us (5%)
  other arithmetic  9.5 us (3%)
  starting transfers between devices  7.23 us (3%)
    all_to_all x1, waiting for transfers between devices, local(): lax.all_to_all(outgoing, 'member', split_axis=0, concat_axis=0, tiled=True)  116 us
    all_gather x1, blocking collectives, local(): lax.all_gather(wanted.reshape(1, requests), 'member', axis=0, tiled=True)  41.5 us
    sub x2, matrix products, attend(): expd = jnp.exp(scores - peak)  25.1 us
    dot_general x2, matrix products, attend(): jnp.einsum('kgts,skd->tkgd', probs, value_block, preferred_element_type=j...  20.9 us
    all_gather x1, blocking collectives, local(): head_columns = lax.all_gather(w_kv, 'group', axis=1, tiled=True)  13.6 us
    dynamic_update_slice x4, local copies, waits for them, and re-layouts, local(): results = lax.map(attend, (queries, keys, values))  8.71 us
    all_to_all x1, starting transfers between devices, local(): lax.all_to_all(outgoing, 'member', split_axis=0, concat_axis=0, tiled=True)  7.23 us
    unnamed x14, local copies, waits for them, and re-layouts  7.19 us
  transfers between devices with their start and end apart: 2, of which 1 were waited for; matrix products, arithmetic and copies ran while one was open for 7% of the time, Pallas kernels for 0%

commit v1 on v0

v1 whole, which is shorter than its diff:
```python
import functools

import jax
import jax.numpy as jnp
from jax import lax
from jax.experimental import pallas as pl
from jax.experimental.pallas import tpu as pltpu
from jax.sharding import PartitionSpec as P

D = 4096
HQ = 64
KVH = 4
HD = 128
TOPP = 8
QLEN = 128
PLEN = 64
RECOMP = 16
KEPT = PLEN - RECOMP
EPSILON = 1e-06
LOG2E = 1.4426950408889634
MESH = pl.DeviceIdType.MESH
NX, NY, NZ = 4, 4, 8
HPB = 2


def comm_kernel(
    cache_ref, hid_ref, w_ref, pos_ref, ret_ref,
    slots_ref, rec_ref,
    blk, wb, hn, acc, stage, recst, info,
    local_sem, wz_s, wz_r, wy_s, wy_r, wx_s, wx_r, wf_s, wf_r,
    in_s, in_r, zr_s, zr_r, zl_s, zl_r, ys_s, ys_r, hx_s, hx_r, rx_s, rx_r,
):
    g, m = lax.axis_index("group"), lax.axis_index("member")
    x, c, y, z = g // 2, g % 2, m // NZ, m % NZ

    def at(dx=0, dc=0, dy=0, dz=0):
        gg = ((x + dx + NX) % NX) * 2 + (c + dc) % 2
        return gg, ((y + dy + NY) % NY) * NZ + (z + dz + NZ) % NZ

    def remote(src, dst, s, r, dev):
        return pltpu.make_async_remote_copy(
            src_ref=src, dst_ref=dst, send_sem=s, recv_sem=r, device_id=dev, device_id_type=MESH
        )

    sends = []

    def go(copy):
        copy.start()
        sends.append(copy)
        return copy

    peers = [at(dz=k) for k in range(1, NZ)] + [at(dy=k) for k in range(1, NY)]
    peers += [at(dx=1), at(dx=-1), at(dc=1)]
    barrier = pltpu.get_barrier_semaphore()
    for dev in peers:
        pl.semaphore_signal(barrier, inc=1, device_id=dev, device_id_type=MESH)

    lane = lax.broadcasted_iota(jnp.int32, (16, 256), 1)
    row = lane % PLEN
    spots = pos_ref[...].reshape(16, RECOMP)
    covered = row == spots[:, 0:1]
    for j in range(1, RECOMP):
        covered = covered | (row == spots[:, j : j + 1])
    free = jnp.where(covered[:, :PLEN], 0.0, 1.0).astype(jnp.bfloat16)
    below = lax.broadcasted_iota(jnp.int32, (PLEN, 256), 0)
    before = below < lax.broadcasted_iota(jnp.int32, (PLEN, 256), 1) % PLEN
    rank = jnp.dot(
        free, jnp.where(before, 1.0, 0.0).astype(jnp.bfloat16), preferred_element_type=jnp.float32
    )
    wanted = ret_ref[...]
    keep = jnp.logical_not(covered) & (lane // PLEN == wanted % 4)
    info[0, :, 0:256] = jnp.where(keep, rank, -1.0)
    info[0, :, 256:512] = jnp.broadcast_to((wanted // 4).astype(jnp.float32), (16, 256))

    pl.semaphore_wait(barrier, len(peers))

    zrow = pl.multiple_of(z * 128, 128)
    for k in range(1, NZ):
        go(remote(w_ref, wb.at[x, y, pl.ds(zrow, 128)], wz_s.at[k], wz_r.at[k], at(dz=k)))
    for k in range(1, NY):
        go(remote(info.at[0], info.at[k], in_s.at[k], in_r.at[k], at(dy=k)))

    def half_right(i):
        return 0 if i == 6 else i % 2

    def half_left(i):
        return 1 if i == 6 else 1 - i % 2

    def zz(d):
        return (z + d + NZ) % NZ

    def right(i):
        h = half_right(i)
        src = cache_ref.at[h] if i < 2 else blk.at[zz(-(i // 2)), h]
        return remote(src, blk.at[zz(-(i // 2)), h], zr_s.at[i], zr_r.at[i], at(dz=1))

    def left(i):
        h = half_left(i)
        src = cache_ref.at[h] if i < 2 else blk.at[zz(i // 2), h]
        return remote(src, blk.at[zz(i // 2), h], zl_s.at[i], zl_r.at[i], at(dz=-1))

    def z_arrived(i):
        d = blk.at[zz(-1 - i // 2), half_right(i)]
        remote(d, d, zr_s.at[i], zr_r.at[i], at(dz=-1)).wait_recv()
        if i + 2 <= 6:
            go(right(i + 2))
        d = blk.at[zz(1 + i // 2), half_left(i)]
        remote(d, d, zl_s.at[i], zl_r.at[i], at(dz=1)).wait_recv()
        if i + 2 <= 6:
            go(left(i + 2))

    for i in range(2):
        go(right(i))
        go(left(i))
    own_block = pltpu.make_async_copy(cache_ref, blk.at[z], local_sem.at[0])
    own_block.start()
    own_w = pltpu.make_async_copy(w_ref, wb.at[x, y, pl.ds(zrow, 128)], local_sem.at[1])
    own_w.start()

    def norm(i, carry):
        rows = pl.ds(pl.multiple_of(i * 32, 32), 32)
        h = hid_ref[rows, :].astype(jnp.float32)
        inv = lax.rsqrt(jnp.mean(h * h, axis=1, keepdims=True) + EPSILON)
        n = (h * inv).astype(jnp.bfloat16)
        for b in range(4):
            hn[b, rows, :] = n[:, b * 1024 : (b + 1) * 1024]
        return carry

    lax.fori_loop(0, 8, norm, 0)
    mine, theirs = pl.ds(0, 256), pl.ds(256, 256)
    go(remote(hn.at[:, mine], hn.at[:, theirs], hx_s, hx_r, at(dc=1)))

    local = []

    def select(d):
        holder = zz(d)
        name = (y * NZ + holder).astype(jnp.float32)
        want = lax.broadcasted_iota(jnp.int32, (KEPT, 256), 0).astype(jnp.float32)
        picks = []
        for k in range(NY):
            hit = info[k, :, 256:512] == name
            v = jnp.max(jnp.where(hit, info[k, :, 0:256], -1.0), axis=0, keepdims=True)
            picks.append(jnp.where(want == v, 1.0, 0.0).astype(jnp.bfloat16))
        got = jnp.dot(
            jnp.concatenate(picks, axis=0),
            blk[holder].reshape(256, 1024),
            preferred_element_type=jnp.float32,
        ).astype(jnp.bfloat16)
        for k in range(NY):
            stage[k, d] = got[k * KEPT : (k + 1) * KEPT]
        slot = slots_ref.at[y * NZ + holder]
        for k in range(1, NY):
            go(remote(stage.at[k, d], slot, ys_s.at[k, d], ys_r.at[k, d], at(dy=-k)))
        mine_too = pltpu.make_async_copy(stage.at[0, d], slot, local_sem.at[4 + d])
        mine_too.start()
        local.append(mine_too)

    started = set()

    def project(dx, k):
        xi, yi = (x + dx + NX) % NX, (y - k + NY) % NY
        part = jnp.dot(hn[yi], wb[xi, yi], preferred_element_type=jnp.float32)
        if dx in started:
            acc[dx] = acc[dx] + part
        else:
            started.add(dx)
            acc[dx] = part

    def chunk(dx, k):
        return wb.at[(x + dx + NX) % NX, (y - k + NY) % NY]

    def wx_send(k):
        go(remote(chunk(0, k), chunk(0, k), wx_s.at[0, k], wx_r.at[0, k], at(dx=1)))
        go(remote(chunk(0, k), chunk(0, k), wx_s.at[1, k], wx_r.at[1, k], at(dx=-1)))

    def wx_arrived(k):
        d = chunk(-1, k)
        remote(d, d, wx_s.at[0, k], wx_r.at[0, k], at(dx=-1)).wait_recv()
        if k in (0, 1):
            go(remote(d, d, wf_s.at[k], wf_r.at[k], at(dx=1)))
        d = chunk(1, k)
        remote(d, d, wx_s.at[1, k], wx_r.at[1, k], at(dx=1)).wait_recv()
        if k in (2, 3):
            go(remote(d, d, wf_s.at[k], wf_r.at[k], at(dx=-1)))
        project(3, k)
        project(1, k)

    def wf_arrived(k):
        d = chunk(2, k)
        remote(d, d, wf_s.at[k], wf_r.at[k], at(dx=-1 if k in (0, 1) else 1)).wait_recv()
        project(2, k)

    def wy_arrived(k):
        d = chunk(0, k)
        remote(d, d, wy_s.at[k], wy_r.at[k], at(dy=-k)).wait_recv()
        wx_send(k)
        project(0, k)

    for k in range(1, NY):
        remote(info.at[k], info.at[k], in_s.at[k], in_r.at[k], at(dy=-k)).wait_recv()
    own_block.wait()
    select(0)

    own_w.wait()
    for k in range(1, NZ):
        d = wb.at[x, y, pl.ds(pl.multiple_of(zz(-k) * 128, 128), 128)]
        remote(d, d, wz_s.at[k], wz_r.at[k], at(dz=-k)).wait_recv()
    wx_send(0)
    for k in range(1, NY):
        go(remote(chunk(0, 0), chunk(0, 0), wy_s.at[k], wy_r.at[k], at(dy=k)))
    remote(hn.at[:, mine], hn.at[:, theirs], hx_s, hx_r, at(dc=1)).wait_recv()
    project(0, 0)

    z_arrived(0)
    wx_arrived(0)
    wy_arrived(1)
    wy_arrived(3)
    z_arrived(1)
    select(7)
    select(1)
    wy_arrived(2)
    wf_arrived(0)
    z_arrived(2)
    wx_arrived(1)
    z_arrived(3)
    select(6)
    select(2)
    wx_arrived(3)
    z_arrived(4)
    wx_arrived(2)
    wf_arrived(1)
    wf_arrived(3)
    z_arrived(5)
    select(5)
    select(3)
    wf_arrived(2)

    for dx in range(NX):
        xi = (x + dx) % NX
        recst[dx] = acc[dx].astype(jnp.bfloat16)
        dst = rec_ref.at[2 * xi + c]
        go(remote(recst.at[dx, theirs], dst, rx_s.at[dx], rx_r.at[dx], at(dc=1)))
        own = pltpu.make_async_copy(recst.at[dx, mine], dst, local_sem.at[12 + dx])
        own.start()
        local.append(own)

    z_arrived(6)
    select(4)

    for k in range(1, NY):
        for d in range(NZ):
            slot = slots_ref.at[((y + k) % NY) * NZ + zz(d)]
            remote(stage.at[k, d], slot, ys_s.at[k, d], ys_r.at[k, d], at(dy=k)).wait_recv()
    for dx in range(NX):
        dst = rec_ref.at[2 * ((x + dx) % NX) + (c + 1) % 2]
        remote(recst.at[dx, theirs], dst, rx_s.at[dx], rx_r.at[dx], at(dc=1)).wait_recv()
    for copy in local:
        copy.wait()
    for copy in sends:
        copy.wait_send()


def attend_kernel(holder_ref, q_ref, own_ref, slots_ref, rec_k_ref, rec_v_ref, out_ref, keys, vals):
    n, h = pl.program_id(0), pl.program_id(1)
    kcol = pl.multiple_of(h * HD, HD)
    vcol = pl.multiple_of(KVH * HD + h * HD, HD)
    cached, span = TOPP * KEPT, TOPP * PLEN + QLEN
    for j in range(TOPP):
        s = holder_ref[n, j]
        keys[j * KEPT : (j + 1) * KEPT, :] = slots_ref[s, :, pl.ds(kcol, HD)]
        vals[j * KEPT : (j + 1) * KEPT, 0:HD] = slots_ref[s, :, pl.ds(vcol, HD)]
    keys[cached : TOPP * PLEN, :] = rec_k_ref[0]
    vals[cached : TOPP * PLEN, 0:HD] = rec_v_ref[0]
    keys[TOPP * PLEN :, :] = own_ref[:, pl.ds(kcol, HD)]
    vals[TOPP * PLEN :, 0:HD] = own_ref[:, pl.ds(vcol, HD)]
    vals[:, HD:] = jnp.ones((span, HD), jnp.bfloat16)

    t = lax.broadcasted_iota(jnp.int32, (HPB * QLEN, QLEN), 0) % QLEN
    seen = lax.broadcasted_iota(jnp.int32, (HPB * QLEN, QLEN), 1) <= t
    factor = LOG2E / HD**0.5

    for b in range(HQ // KVH // HPB):
        heads = [b * HPB + i for i in range(HPB)]
        q = jnp.concatenate([q_ref[:, i * HD : (i + 1) * HD] for i in heads], axis=0)
        s = lax.dot_general(
            q, keys[...], (((1,), (1,)), ((), ())), preferred_element_type=jnp.float32
        )
        s_own = jnp.where(seen, s[:, TOPP * PLEN :], -jnp.inf)
        s = jnp.concatenate([s[:, : TOPP * PLEN], s_own], axis=1)
        peak = jnp.max(s, axis=1, keepdims=True)
        p = jnp.exp2((s - peak) * factor).astype(jnp.bfloat16)
        o = jnp.dot(p, vals[...], preferred_element_type=jnp.float32)
        o = (o[:, :HD] / o[:, HD:]).astype(jnp.bfloat16)
        for i, hd in enumerate(heads):
            out_ref[:, hd * HD : (hd + 1) * HD] = o[i * QLEN : (i + 1) * QLEN]


def communicate(cache, hidden, w_kv, positions, wanted):
    dma, bf, f32 = pltpu.SemaphoreType.DMA, jnp.bfloat16, jnp.float32
    vmem, hbm = pl.BlockSpec(memory_space=pltpu.VMEM), pl.BlockSpec(memory_space=pl.ANY)
    return pl.pallas_call(
        comm_kernel,
        out_shape=(
            jax.ShapeDtypeStruct((NY * NZ, KEPT, 1024), bf),
            jax.ShapeDtypeStruct((8, 256, 128), bf),
        ),
        in_specs=[hbm, vmem, vmem, vmem, vmem],
        out_specs=(hbm, hbm),
        scratch_shapes=[
            pltpu.VMEM((NZ, 2, 128, 1024), bf),
            pltpu.VMEM((NX, NY, 1024, 128), bf),
            pltpu.VMEM((4, 512, 1024), bf),
            pltpu.VMEM((NX, 512, 128), f32),
            pltpu.VMEM((NY, NZ, KEPT, 1024), bf),
            pltpu.VMEM((NX, 512, 128), bf),
            pltpu.VMEM((NY, 16, 512), f32),
            dma((16,)),
            dma((NZ,)), dma((NZ,)), dma((NY,)), dma((NY,)),
            dma((2, NY)), dma((2, NY)), dma((NY,)), dma((NY,)),
            dma((NY,)), dma((NY,)), dma((7,)), dma((7,)), dma((7,)), dma((7,)),
            dma((NY, NZ)), dma((NY, NZ)), dma, dma, dma((NX,)), dma((NX,)),
        ],
        compiler_params=pltpu.CompilerParams(
            collective_id=0, has_side_effects=True, vmem_limit_bytes=48 << 20
        ),
        name="exchange",
    )(cache, hidden, w_kv, positions, wanted)


def attend(holders, q, own, slots, rec):
    width = HQ // KVH * HD
    return pl.pallas_call(
        attend_kernel,
        out_shape=jax.ShapeDtypeStruct(q.shape, q.dtype),
        grid_spec=pltpu.PrefetchScalarGridSpec(
            num_scalar_prefetch=1,
            grid=(q.shape[0] // QLEN, KVH),
            in_specs=[
                pl.BlockSpec((QLEN, width), lambda n, h, s: (n, h)),
                pl.BlockSpec((QLEN, 1024), lambda n, h, s: (n, 0)),
                pl.BlockSpec((NY * NZ, KEPT, 1024), lambda n, h, s: (0, 0, 0)),
                pl.BlockSpec((1, QLEN, HD), lambda n, h, s: (h, n, 0)),
                pl.BlockSpec((1, QLEN, HD), lambda n, h, s: (h + KVH, n, 0)),
            ],
            out_specs=pl.BlockSpec((QLEN, width), lambda n, h, s: (n, h)),
            scratch_shapes=[
                pltpu.VMEM((TOPP * PLEN + QLEN, HD), jnp.bfloat16),
                pltpu.VMEM((TOPP * PLEN + QLEN, 2 * HD), jnp.bfloat16),
            ],
        ),
        compiler_params=pltpu.CompilerParams(vmem_limit_bytes=48 << 20),
        name="attend",
    )(holders, q, own, slots, rec, rec)


def local(q_rows, own_kv, cache, recomp_hidden, w_kv, retrieval, positions):
    slots, rec = communicate(
        cache.reshape(2, 128, 1024),
        recomp_hidden.reshape(256, D),
        w_kv,
        positions,
        retrieval.reshape(16, 1),
    )
    return attend(retrieval // 4, q_rows, own_kv, slots, rec)


def solution(mesh):
    both = ("group", "member")
    placed = (
        P(both, None),
        P(both, None),
        P(both, None, None),
        P(both, None, None, None),
        P("member", "group"),
        P(both, None),
        P(both, None, None),
    )
    return jax.shard_map(
        local, mesh=mesh, in_specs=placed, out_specs=P(both, None), check_vma=False
    )
```

time: 288 us -> 103 us (0.36)
  waiting for transfers between devices: 116 us -> 0 us
  Pallas kernels: 0 us -> 93.8 us
  matrix products: 55.1 us -> 0 us
  blocking collectives: 55.1 us -> 0 us
  local copies, waits for them, and re-layouts: 29.1 us -> 7.77 us
  between operations: 13.5 us -> 0.02 us
  other arithmetic: 9.5 us -> 0.69 us
  starting transfers between devices: 7.23 us -> 0 us
    all_to_all x1 -> x0, waiting for transfers between devices: 116 us -> none  [local(): lax.all_to_all(outgoing, 'member', split_axis=0, concat_axis=0, tiled=True)]
    pallas_call x0 -> x2, Pallas kernels: none -> 93.8 us  [the longest x1 68.8 us: communicate(): pl.pallas_call(comm_kernel, out_shape=(jax.ShapeDtypeStruct((NY * NZ, KEP...]
    all_gather x2 -> x0, blocking collectives: 55.1 us -> none  [the longest x1 41.5 us: local(): lax.all_gather(wanted.reshape(1, requests), 'member', axis=0, tiled=True)]
    dot_general x5 -> x0, matrix products: 30 us -> none  [the longest x2 20.9 us: attend(): jnp.einsum('kgts,skd->tkgd', probs, value_block, preferred_element_type=j...]
    sub x2 -> x0, matrix products: 25.1 us -> none  [attend(): expd = jnp.exp(scores - peak)]
    dynamic_update_slice x4 -> x0, local copies, waits for them, and re-layouts: 8.71 us -> none  [local(): results = lax.map(attend, (queries, keys, values))]
    all_to_all x1 -> x0, starting transfers between devices: 7.23 us -> none  [local(): lax.all_to_all(outgoing, 'member', split_axis=0, concat_axis=0, tiled=True)]
    gather x2 -> x0, local copies, waits for them, and re-layouts: 5.7 us -> none  [the longest x1 2.87 us: local(): arrived.reshape(holders_count * capacity, PLEN, kv_width)]
  transfers between devices with their start and end apart: 2 -> 0, of which waited for: 1 -> 0; matrix products, arithmetic and copies ran while one was open for 7% -> 0% of each run, Pallas kernels for 0% -> 0%
where the time goes in v1:
time: 103 us; the launch traced here: 102 us
  Pallas kernels  93.8 us (91%)
  local copies, waits for them, and re-layouts  7.77 us (8%)
    pallas_call x1, Pallas kernels, communicate(): pl.pallas_call(comm_kernel, out_shape=(jax.ShapeDtypeStruct((NY * NZ, KEP...  68.8 us
    pallas_call x1, Pallas kernels, attend(): pl.pallas_call(attend_kernel, out_shape=jax.ShapeDtypeStruct(q.shape, q.d...  25 us
    unnamed x12, local copies, waits for them, and re-layouts  7.01 us

profile of v1, /device:TPU:8, one launch (start us, length us, event | category | flops | bytes accessed | tf_op | source)
XLA Modules:
  0.0 102.2 jit_solution(7578323497110316702)
XLA Ops:
  0.0 0.7 and_select_fusion.holder_ref
  0.7 0.8 reshape.12.ret_ref
  1.4 0.0 copy-start.1
  1.4 1.6 %copy-done.1 = bf16[2,8,16,4096]{3,2,1,0:T(8,128)(2,1)S(1)} copy-done((bf16[2,8,16,4096]{3,2,1,0:T(8,128)(2,1)S(1)}, bf16[2,8,16,4096]{3,2,1,0:T(8,128)(2,1)}, u32[]{:S(2)}) %copy-start.1) | copy-done | bytes 2097176
  3.0 0.0 copy-start.2
  3.0 1.0 %copy-done.2 = bf16[4,64,1024]{2,1,0:T(8,128)(2,1)S(1)} copy-done((bf16[4,64,1024]{2,1,0:T(8,128)(2,1)S(1)}, bf16[4,64,1024]{2,1,0:T(8,128)(2,1)}, u32[]{:S(2)}) %copy-start.2) | copy-done | bytes 524312
  4.1 0.0 copy-start.4
  4.1 0.8 copy-done.4
  4.8 0.0 copy-start.5
  4.8 0.7 copy-done.5
  5.5 68.8 %exchange.1 = (bf16[32,48,1024]{2,1,0:T(8,128)(2,1)}, bf16[8,256,128]{2,1,0:T(8,128)(2,1)S(1)}) custom-call(bf16[2,128,1024]{2,1,0:T(8,128)(2,1)S(1)} %bitcast.3, bf16[256,4096]{1,0:T(8,128)(2,1)S(1)} %bitcast.2, bf16[128,128]{1,0:T(8,128)(2,1)S(1)} %copy-done.4, s32[2,8,16]{2,1,0:T(8,128)S(1)} %copy-done.5, s32[16,1]{1,0:T(8,128)S(1)} %reshape.12.ret_ref), custom_call_target="tpu_custom_call" | custom-call | tf_op jit(solution)/shard_map/exchange/pallas_call | solution.py:301
  74.3 0.0 copy-start
  74.3 1.9 %copy-done = bf16[32,48,1024]{2,1,0:T(8,128)(2,1)S(1)} copy-done((bf16[32,48,1024]{2,1,0:T(8,128)(2,1)S(1)}, bf16[32,48,1024]{2,1,0:T(8,128)(2,1)}, u32[]{:S(2)}) %copy-start) | copy-done | bytes 3145752
  76.2 0.0 copy-start.3
  76.2 1.0 %copy-done.3 = bf16[256,1024]{1,0:T(8,128)(2,1)S(1)} copy-done((bf16[256,1024]{1,0:T(8,128)(2,1)S(1)}, bf16[256,1024]{1,0:T(8,128)(2,1)}, u32[]{:S(2)}) %copy-start.3) | copy-done | bytes 524312
  77.2 25.0 %attend.1 = bf16[256,8192]{1,0:T(8,128)(2,1)} custom-call(s32[2,8]{1,0:T(2,128)S(1)} %and_select_fusion.holder_ref, bf16[256,8192]{1,0:T(8,128)(2,1)} %q_ref.1, bf16[256,1024]{1,0:T(8,128)(2,1)S(1)} %copy-done.3, bf16[32,48,1024]{2,1,0:T(8,128)(2,1)S(1)} %copy-done, bf16[8,256,128]{2,1,0:T(8,128)(2,1)S(1)} %get-tuple-element.8.rec_k_ref.rec_v_ref, ...), custom_call_target="tpu_custom_call" | custom-call | tf_op jit(solution)/shard_map/attend/pallas_call | solution.py:332
Async XLA Ops:
  1.4 1.6 %copy-start.1 = (bf16[2,8,16,4096]{3,2,1,0:T(8,128)(2,1)S(1)}, bf16[2,8,16,4096]{3,2,1,0:T(8,128)(2,1)}, u32[]{:S(2)}) copy-start(bf16[2,8,16,4096]{3,2,1,0:T(8,128)(2,1)} %param.10) | copy-start | bytes 6291460
  3.0 1.0 %copy-start.2 = (bf16[4,64,1024]{2,1,0:T(8,128)(2,1)S(1)}, bf16[4,64,1024]{2,1,0:T(8,128)(2,1)}, u32[]{:S(2)}) copy-start(bf16[4,64,1024]{2,1,0:T(8,128)(2,1)} %param.9) | copy-start | bytes 1572868
  4.1 0.8 copy-start.4
  4.8 0.7 copy-start.5
  74.3 1.9 %copy-start = (bf16[32,48,1024]{2,1,0:T(8,128)(2,1)S(1)}, bf16[32,48,1024]{2,1,0:T(8,128)(2,1)}, u32[]{:S(2)}) copy-start(bf16[32,48,1024]{2,1,0:T(8,128)(2,1)} %get-tuple-element.7.slots_ref) | copy-start | bytes 9437188
  76.2 1.0 %copy-start.3 = (bf16[256,1024]{1,0:T(8,128)(2,1)S(1)}, bf16[256,1024]{1,0:T(8,128)(2,1)}, u32[]{:S(2)}) copy-start(bf16[256,1024]{1,0:T(8,128)(2,1)} %own_ref.1) | copy-start | bytes 1572868

commit v2 on v1

--- a/solution.py
+++ b/solution.py
@@ -20,14 +20,17 @@
 LOG2E = 1.4426950408889634
 MESH = pl.DeviceIdType.MESH
 NX, NY, NZ = 4, 4, 8
-HPB = 2
+HPB = 8
+GROUPED = HQ // KVH
+WIDTH = GROUPED * HD
+FACTOR = LOG2E / HD**0.5
 
 
 def comm_kernel(
-    cache_ref, hid_ref, w_ref, pos_ref, ret_ref,
-    slots_ref, rec_ref,
-    blk, wb, hn, acc, stage, recst, info,
-    local_sem, wz_s, wz_r, wy_s, wy_r, wx_s, wx_r, wf_s, wf_r,
+    ret_ref, cache_ref, hid_hbm, w_ref, pos_hbm, q_hbm, own_hbm,
+    slots_ref, rec_ref, part_ref, lse_ref,
+    blk, wb, hn, acc, stage, recst, info, hid_ref, pos_ref, queries, own_ref, ones, part, lse,
+    local_sem, in_sem, q_sem, part_sem, lse_sem, wz_s, wz_r, wy_s, wy_r, wx_s, wx_r, wf_s, wf_r,
     in_s, in_r, zr_s, zr_r, zl_s, zl_r, ys_s, ys_r, hx_s, hx_r, rx_s, rx_r,
 ):
     g, m = lax.axis_index("group"), lax.axis_index("member")
@@ -48,6 +51,15 @@
         copy.start()
         sends.append(copy)
         return copy
+
+    loads = [
+        pltpu.make_async_copy(src, dst, in_sem.at[i])
+        for i, (src, dst) in enumerate(((pos_hbm, pos_ref), (own_hbm, own_ref), (hid_hbm, hid_ref)))
+    ]
+
+    def query(n, h):
+        block = (pl.ds(n * QLEN, QLEN), pl.ds(h * WIDTH, WIDTH))
+        return pltpu.make_async_copy(q_hbm.at[block], queries.at[block], q_sem.at[n, h])
 
     peers = [at(dz=k) for k in range(1, NZ)] + [at(dy=k) for k in range(1, NY)]
     peers += [at(dx=1), at(dx=-1), at(dc=1)]
@@ -55,8 +67,15 @@
     for dev in peers:
         pl.semaphore_signal(barrier, inc=1, device_id=dev, device_id_type=MESH)
 
+    for copy in loads:
+        copy.start()
+    for n in range(2):
+        for h in range(KVH):
+            query(n, h).start()
+
     lane = lax.broadcasted_iota(jnp.int32, (16, 256), 1)
     row = lane % PLEN
+    loads[0].wait()
     spots = pos_ref[...].reshape(16, RECOMP)
     covered = row == spots[:, 0:1]
     for j in range(1, RECOMP):
@@ -67,10 +86,13 @@
     rank = jnp.dot(
         free, jnp.where(before, 1.0, 0.0).astype(jnp.bfloat16), preferred_element_type=jnp.float32
     )
-    wanted = ret_ref[...]
+    request = lax.broadcasted_iota(jnp.int32, (16, 256), 0)
+    wanted = jnp.zeros((16, 256), jnp.int32)
+    for k in range(16):
+        wanted = jnp.where(request == k, ret_ref[k // TOPP, k % TOPP], wanted)
     keep = jnp.logical_not(covered) & (lane // PLEN == wanted % 4)
     info[0, :, 0:256] = jnp.where(keep, rank, -1.0)
-    info[0, :, 256:512] = jnp.broadcast_to((wanted // 4).astype(jnp.float32), (16, 256))
+    info[0, :, 256:512] = (wanted // 4).astype(jnp.float32)
 
     pl.semaphore_wait(barrier, len(peers))
 
@@ -117,6 +139,7 @@
     own_w = pltpu.make_async_copy(w_ref, wb.at[x, y, pl.ds(zrow, 128)], local_sem.at[1])
     own_w.start()
 
+    loads[2].wait()
     def norm(i, carry):
         rows = pl.ds(pl.multiple_of(i * 32, 32), 32)
         h = hid_ref[rows, :].astype(jnp.float32)
@@ -196,6 +219,41 @@
         wx_send(k)
         project(0, k)
 
+    loads[1].wait()
+    ones[:, HD:] = jnp.ones((QLEN, HD), jnp.bfloat16)
+    token = lax.broadcasted_iota(jnp.int32, (HPB * QLEN, QLEN), 0) % QLEN
+    seen = lax.broadcasted_iota(jnp.int32, (HPB * QLEN, QLEN), 1) <= token
+    place = lax.broadcasted_iota(jnp.int32, (QLEN, HD), 1)
+
+    def attend_own(n, h):
+        query(n, h).wait()
+        rows = slice(n * QLEN, (n + 1) * QLEN)
+        key = own_ref[rows, h * HD : (h + 1) * HD]
+        ones[:, :HD] = own_ref[rows, (KVH + h) * HD : (KVH + h + 1) * HD]
+        packed = jnp.zeros((QLEN, HD), jnp.float32)
+        for b in range(GROUPED // HPB):
+            cols = [h * WIDTH + (b * HPB + i) * HD for i in range(HPB)]
+            q = jnp.concatenate([queries[rows, a : a + HD] for a in cols], axis=0)
+            s = lax.dot_general(q, key, (((1,), (1,)), ((), ())), preferred_element_type=jnp.float32)
+            s = jnp.where(seen, s, -jnp.inf)
+            peak = jnp.max(s, axis=1, keepdims=True)
+            p = jnp.exp2((s - peak) * FACTOR).astype(jnp.bfloat16)
+            o = jnp.dot(p, ones[...], preferred_element_type=jnp.float32)
+            total = o[:, HD:]
+            o = (o[:, :HD] / total).astype(jnp.bfloat16)
+            score = peak + jnp.log2(total) / FACTOR
+            for i, a in enumerate(cols):
+                part[rows, a : a + HD] = o[i * QLEN : (i + 1) * QLEN]
+                packed = jnp.where(place == b * HPB + i, score[i * QLEN : (i + 1) * QLEN], packed)
+        lse[n, h] = packed
+        block = (pl.ds(n * QLEN, QLEN), pl.ds(h * WIDTH, WIDTH))
+        for copy in (
+            pltpu.make_async_copy(part.at[block], part_ref.at[block], part_sem.at[n, h]),
+            pltpu.make_async_copy(lse.at[n, h], lse_ref.at[n, h], lse_sem.at[n, h]),
+        ):
+            copy.start()
+            local.append(copy)
+
     for k in range(1, NY):
         remote(info.at[k], info.at[k], in_s.at[k], in_r.at[k], at(dy=-k)).wait_recv()
     own_block.wait()
@@ -211,8 +269,10 @@
     remote(hn.at[:, mine], hn.at[:, theirs], hx_s, hx_r, at(dc=1)).wait_recv()
     project(0, 0)
 
+    attend_own(0, 0)
     z_arrived(0)
     wx_arrived(0)
+    attend_own(0, 1)
     wy_arrived(1)
     wy_arrived(3)
     z_arrived(1)
@@ -220,16 +280,22 @@
     select(1)
     wy_arrived(2)
     wf_arrived(0)
+    attend_own(0, 2)
     z_arrived(2)
+    attend_own(0, 3)
     wx_arrived(1)
     z_arrived(3)
     select(6)
     select(2)
+    attend_own(1, 0)
     wx_arrived(3)
+    attend_own(1, 1)
     z_arrived(4)
     wx_arrived(2)
+    attend_own(1, 2)
     wf_arrived(1)
     wf_arrived(3)
+    attend_own(1, 3)
     z_arrived(5)
     select(5)
     select(3)
@@ -260,52 +326,72 @@
         copy.wait_send()
 
 
-def attend_kernel(holder_ref, q_ref, own_ref, slots_ref, rec_k_ref, rec_v_ref, out_ref, keys, vals):
+def attend_kernel(ret_ref, q_ref, part_ref, lse_ref, slots_hbm, rec_hbm, out_ref, ctx, vals, sem):
     n, h = pl.program_id(0), pl.program_id(1)
-    kcol = pl.multiple_of(h * HD, HD)
-    vcol = pl.multiple_of(KVH * HD + h * HD, HD)
-    cached, span = TOPP * KEPT, TOPP * PLEN + QLEN
-    for j in range(TOPP):
-        s = holder_ref[n, j]
-        keys[j * KEPT : (j + 1) * KEPT, :] = slots_ref[s, :, pl.ds(kcol, HD)]
-        vals[j * KEPT : (j + 1) * KEPT, 0:HD] = slots_ref[s, :, pl.ds(vcol, HD)]
-    keys[cached : TOPP * PLEN, :] = rec_k_ref[0]
-    vals[cached : TOPP * PLEN, 0:HD] = rec_v_ref[0]
-    keys[TOPP * PLEN :, :] = own_ref[:, pl.ds(kcol, HD)]
-    vals[TOPP * PLEN :, 0:HD] = own_ref[:, pl.ds(vcol, HD)]
-    vals[:, HD:] = jnp.ones((span, HD), jnp.bfloat16)
-
-    t = lax.broadcasted_iota(jnp.int32, (HPB * QLEN, QLEN), 0) % QLEN
-    seen = lax.broadcasted_iota(jnp.int32, (HPB * QLEN, QLEN), 1) <= t
-    factor = LOG2E / HD**0.5
-
-    for b in range(HQ // KVH // HPB):
+    cached = TOPP * KEPT
+
+    def fetch(i):
+        copies = [
+            pltpu.make_async_copy(
+                slots_hbm.at[ret_ref[i, j] // 4], ctx.at[i, pl.ds(j * KEPT, KEPT)], sem.at[i, j]
+            )
+            for j in range(TOPP)
+        ]
+        return copies + [
+            pltpu.make_async_copy(
+                rec_hbm.at[e, pl.ds(i * QLEN, QLEN)],
+                ctx.at[i, pl.ds(cached, QLEN), pl.ds(e * HD, HD)],
+                sem.at[i, TOPP + e],
+            )
+            for e in range(2 * KVH)
+        ]
+
+    for i in range(2):
+
+        @pl.when((n == 0) & (h == 0))
+        def _():
+            for copy in fetch(i):
+                copy.start()
+
+    for i in range(2):
+
+        @pl.when((n == i) & (h == 0))
+        def _():
+            for copy in fetch(i):
+                copy.wait()
+            vals[:, HD:] = jnp.ones((TOPP * PLEN, HD), jnp.bfloat16)
+
+    key = ctx[n, :, pl.ds(pl.multiple_of(h * HD, HD), HD)]
+    vals[:, :HD] = ctx[n, :, pl.ds(pl.multiple_of((KVH + h) * HD, HD), HD)]
+    for b in range(GROUPED // HPB):
         heads = [b * HPB + i for i in range(HPB)]
         q = jnp.concatenate([q_ref[:, i * HD : (i + 1) * HD] for i in heads], axis=0)
-        s = lax.dot_general(
-            q, keys[...], (((1,), (1,)), ((), ())), preferred_element_type=jnp.float32
-        )
-        s_own = jnp.where(seen, s[:, TOPP * PLEN :], -jnp.inf)
-        s = jnp.concatenate([s[:, : TOPP * PLEN], s_own], axis=1)
-        peak = jnp.max(s, axis=1, keepdims=True)
-        p = jnp.exp2((s - peak) * factor).astype(jnp.bfloat16)
+        own = jnp.concatenate([lse_ref[0, 0, :, i : i + 1] for i in heads], axis=0)
+        s = lax.dot_general(q, key, (((1,), (1,)), ((), ())), preferred_element_type=jnp.float32)
+        peak = jnp.maximum(jnp.max(s, axis=1, keepdims=True), own)
+        p = jnp.exp2((s - peak) * FACTOR).astype(jnp.bfloat16)
+        weight = jnp.exp2((own - peak) * FACTOR)
         o = jnp.dot(p, vals[...], preferred_element_type=jnp.float32)
-        o = (o[:, :HD] / o[:, HD:]).astype(jnp.bfloat16)
         for i, hd in enumerate(heads):
-            out_ref[:, hd * HD : (hd + 1) * HD] = o[i * QLEN : (i + 1) * QLEN]
-
-
-def communicate(cache, hidden, w_kv, positions, wanted):
+            rows, cols = slice(i * QLEN, (i + 1) * QLEN), slice(hd * HD, (hd + 1) * HD)
+            w = weight[rows]
+            top = o[rows, :HD] + w * part_ref[:, cols].astype(jnp.float32)
+            out_ref[:, cols] = (top / (o[rows, HD:] + w)).astype(jnp.bfloat16)
+
+
+def communicate(retrieval, cache, hidden, w_kv, positions, q, own):
     dma, bf, f32 = pltpu.SemaphoreType.DMA, jnp.bfloat16, jnp.float32
-    vmem, hbm = pl.BlockSpec(memory_space=pltpu.VMEM), pl.BlockSpec(memory_space=pl.ANY)
+    hbm = pl.BlockSpec(memory_space=pltpu.HBM)
     return pl.pallas_call(
         comm_kernel,
         out_shape=(
             jax.ShapeDtypeStruct((NY * NZ, KEPT, 1024), bf),
             jax.ShapeDtypeStruct((8, 256, 128), bf),
+            jax.ShapeDtypeStruct(q.shape, bf),
+            jax.ShapeDtypeStruct((2, KVH, QLEN, HD), f32),
         ),
-        in_specs=[hbm, vmem, vmem, vmem, vmem],
-        out_specs=(hbm, hbm),
+        in_specs=[pl.BlockSpec(memory_space=pltpu.SMEM)] + [hbm] * 6,
+        out_specs=(hbm,) * 4,
         scratch_shapes=[
             pltpu.VMEM((NZ, 2, 128, 1024), bf),
             pltpu.VMEM((NX, NY, 1024, 128), bf),
@@ -314,54 +400,65 @@
             pltpu.VMEM((NY, NZ, KEPT, 1024), bf),
             pltpu.VMEM((NX, 512, 128), bf),
             pltpu.VMEM((NY, 16, 512), f32),
-            dma((16,)),
+            pltpu.VMEM(hidden.shape, bf),
+            pltpu.VMEM(positions.shape, jnp.int32),
+            pltpu.VMEM(q.shape, bf),
+            pltpu.VMEM(own.shape, bf),
+            pltpu.VMEM((QLEN, 2 * HD), bf),
+            pltpu.VMEM(q.shape, bf),
+            pltpu.VMEM((2, KVH, QLEN, HD), f32),
+            dma((16,)), dma((3,)), dma((2, KVH)), dma((2, KVH)), dma((2, KVH)),
             dma((NZ,)), dma((NZ,)), dma((NY,)), dma((NY,)),
             dma((2, NY)), dma((2, NY)), dma((NY,)), dma((NY,)),
             dma((NY,)), dma((NY,)), dma((7,)), dma((7,)), dma((7,)), dma((7,)),
             dma((NY, NZ)), dma((NY, NZ)), dma, dma, dma((NX,)), dma((NX,)),
         ],
         compiler_params=pltpu.CompilerParams(
-            collective_id=0, has_side_effects=True, vmem_limit_bytes=48 << 20
+            collective_id=0, has_side_effects=True, vmem_limit_bytes=56 << 20
         ),
         name="exchange",
-    )(cache, hidden, w_kv, positions, wanted)
-
-
-def attend(holders, q, own, slots, rec):
-    width = HQ // KVH * HD
+    )(retrieval, cache, hidden, w_kv, positions, q, own)
+
+
+def attend(retrieval, q, part, lse, slots, rec):
+    hbm = pl.BlockSpec(memory_space=pltpu.HBM)
+    wide = pl.BlockSpec((QLEN, WIDTH), lambda n, h, s: (n, h))
     return pl.pallas_call(
         attend_kernel,
         out_shape=jax.ShapeDtypeStruct(q.shape, q.dtype),
         grid_spec=pltpu.PrefetchScalarGridSpec(
             num_scalar_prefetch=1,
-            grid=(q.shape[0] // QLEN, KVH),
+            grid=(2, KVH),
             in_specs=[
-                pl.BlockSpec((QLEN, width), lambda n, h, s: (n, h)),
-                pl.BlockSpec((QLEN, 1024), lambda n, h, s: (n, 0)),
-                pl.BlockSpec((NY * NZ, KEPT, 1024), lambda n, h, s: (0, 0, 0)),
-                pl.BlockSpec((1, QLEN, HD), lambda n, h, s: (h, n, 0)),
-                pl.BlockSpec((1, QLEN, HD), lambda n, h, s: (h + KVH, n, 0)),
+                wide,
+                wide,
+                pl.BlockSpec((1, 1, QLEN, HD), lambda n, h, s: (n, h, 0, 0)),
+                hbm,
+                hbm,
             ],
-            out_specs=pl.BlockSpec((QLEN, width), lambda n, h, s: (n, h)),
+            out_specs=wide,
             scratch_shapes=[
-                pltpu.VMEM((TOPP * PLEN + QLEN, HD), jnp.bfloat16),
-                pltpu.VMEM((TOPP * PLEN + QLEN, 2 * HD), jnp.bfloat16),
+                pltpu.VMEM((2, TOPP * PLEN, 1024), jnp.bfloat16),
+                pltpu.VMEM((TOPP * PLEN, 2 * HD), jnp.bfloat16),
+                pltpu.SemaphoreType.DMA((2, 16)),
             ],
         ),
-        compiler_params=pltpu.CompilerParams(vmem_limit_bytes=48 << 20),
+        compiler_params=pltpu.CompilerParams(vmem_limit_bytes=56 << 20),
         name="attend",
-    )(holders, q, own, slots, rec, rec)
+    )(retrieval, q, part, lse, slots, rec)
 
 
 def local(q_rows, own_kv, cache, recomp_hidden, w_kv, retrieval, positions):
-    slots, rec = communicate(
+    slots, rec, part, lse = communicate(
+        retrieval,
         cache.reshape(2, 128, 1024),
         recomp_hidden.reshape(256, D),
         w_kv,
         positions,
-        retrieval.reshape(16, 1),
+        q_rows,
+        own_kv,
     )
-    return attend(retrieval // 4, q_rows, own_kv, slots, rec)
+    return attend(retrieval, q_rows, part, lse, slots, rec)
 
 
 def solution(mesh):

time: 103 us -> 102 us (level)
  Pallas kernels: 93.8 us -> 102 us
  local copies, waits for them, and re-layouts: 7.77 us -> 0 us
    unnamed x12 -> x0, local copies, waits for them, and re-layouts: 7.01 us -> none
    pallas_call x1, Pallas kernels: 25 us -> 30.8 us  [attend(): pl.pallas_call(attend_kernel, out_shape=jax.ShapeDtypeStruct(q.shape, q.d...]
    pallas_call x1, Pallas kernels: 68.8 us -> 71.1 us  [communicate(): pl.pallas_call(comm_kernel, out_shape=(jax.ShapeDtypeStruct((NY * NZ, KEP...]
where the time goes in v2:
time: 102 us
  Pallas kernels  102 us (100%)
    pallas_call x1, Pallas kernels, communicate(): pl.pallas_call(comm_kernel, out_shape=(jax.ShapeDtypeStruct((NY * NZ, KEP...  71.1 us
    pallas_call x1, Pallas kernels, attend(): pl.pallas_call(attend_kernel, out_shape=jax.ShapeDtypeStruct(q.shape, q.d...  30.8 us

profile of v2, /device:TPU:8, one launch (start us, length us, event | category | flops | bytes accessed | tf_op | source)
XLA Modules:
  0.0 102.0 jit_solution(5524338598557254829)
XLA Ops:
  0.0 71.1 %exchange.1 = (bf16[32,48,1024]{2,1,0:T(8,128)(2,1)}, bf16[8,256,128]{2,1,0:T(8,128)(2,1)}, bf16[256,8192]{1,0:T(8,128)(2,1)}, f32[2,4,128,128]{3,2,1,0:T(8,128)}) custom-call(s32[2,8]{1,0:T(2,128)} %ret_ref.3, bf16[2,128,1024]{2,1,0:T(8,128)(2,1)} %bitcast.3, bf16[256,4096]{1,0:T(8,128)(2,1)} %bitcast.2, bf16[128,128]{1,0:T(8,128)(2,1)} %w_ref.1, ...), custom_call_target="tpu_custom_call" | custom-call | tf_op jit(solution)/shard_map/exchange/pallas_call | solution.py:385
  71.1 30.8 %attend.1 = bf16[256,8192]{1,0:T(8,128)(2,1)} custom-call(s32[2,8]{1,0:T(2,128)} %ret_ref.3, bf16[256,8192]{1,0:T(8,128)(2,1)} %q_ref.1, bf16[256,8192]{1,0:T(8,128)(2,1)} %get-tuple-element.9.part_ref, f32[2,4,128,128]{3,2,1,0:T(8,128)} %get-tuple-element.10.lse_ref, bf16[32,48,1024]{2,1,0:T(8,128)(2,1)} %get-tuple-element.11.slots_hbm, ...), custom_call_target="tpu_custom_call" | custom-call | tf_op jit(solution)/shard_map/attend/pallas_call | solution.py:426

commit v3 on v2

--- a/solution.py
+++ b/solution.py
@@ -21,6 +21,8 @@
 MESH = pl.DeviceIdType.MESH
 NX, NY, NZ = 4, 4, 8
 HPB = 8
+HPA = 4
+HALF = KVH * HD
 GROUPED = HQ // KVH
 WIDTH = GROUPED * HD
 FACTOR = LOG2E / HD**0.5
@@ -29,8 +31,8 @@
 def comm_kernel(
     ret_ref, cache_ref, hid_hbm, w_ref, pos_hbm, q_hbm, own_hbm,
     slots_ref, rec_ref, part_ref, lse_ref,
-    blk, wb, hn, acc, stage, recst, info, hid_ref, pos_ref, queries, own_ref, ones, part, lse,
-    local_sem, in_sem, q_sem, part_sem, lse_sem, wz_s, wz_r, wy_s, wy_r, wx_s, wx_r, wf_s, wf_r,
+    blk, wb, hn, acc, stage, recst, info, picks, hid_ref, pos_ref, queries, own_ref, ones, part, lse,
+    local_sem, in_sem, q_sem, part_sem, lse_sem, keep_sem, wz_s, wz_r, wy_s, wy_r, wx_s, wx_r, wf_s, wf_r,
     in_s, in_r, zr_s, zr_r, zl_s, zl_r, ys_s, ys_r, hx_s, hx_r, rx_s, rx_r,
 ):
     g, m = lax.axis_index("group"), lax.axis_index("member")
@@ -111,15 +113,18 @@
     def zz(d):
         return (z + d + NZ) % NZ
 
+    def own_half(h):
+        return cache_ref.at[:, pl.ds(h * HALF, HALF)]
+
     def right(i):
         h = half_right(i)
-        src = cache_ref.at[h] if i < 2 else blk.at[zz(-(i // 2)), h]
-        return remote(src, blk.at[zz(-(i // 2)), h], zr_s.at[i], zr_r.at[i], at(dz=1))
+        dst = blk.at[zz(-(i // 2)), h]
+        return remote(own_half(h) if i < 2 else dst, dst, zr_s.at[i], zr_r.at[i], at(dz=1))
 
     def left(i):
         h = half_left(i)
-        src = cache_ref.at[h] if i < 2 else blk.at[zz(i // 2), h]
-        return remote(src, blk.at[zz(i // 2), h], zl_s.at[i], zl_r.at[i], at(dz=-1))
+        dst = blk.at[zz(i // 2), h]
+        return remote(own_half(h) if i < 2 else dst, dst, zl_s.at[i], zl_r.at[i], at(dz=-1))
 
     def z_arrived(i):
         d = blk.at[zz(-1 - i // 2), half_right(i)]
@@ -130,14 +135,16 @@
         remote(d, d, zl_s.at[i], zl_r.at[i], at(dz=1)).wait_recv()
         if i + 2 <= 6:
             go(left(i + 2))
-
-    for i in range(2):
-        go(right(i))
-        go(left(i))
-    own_block = pltpu.make_async_copy(cache_ref, blk.at[z], local_sem.at[0])
-    own_block.start()
+        select(-1 - i // 2, half_right(i))
+        select(1 + i // 2, half_left(i))
+
     own_w = pltpu.make_async_copy(w_ref, wb.at[x, y, pl.ds(zrow, 128)], local_sem.at[1])
     own_w.start()
+    own_block = [
+        pltpu.make_async_copy(own_half(h), blk.at[z, h], local_sem.at[2 + h]) for h in range(2)
+    ]
+    for copy in own_block:
+        copy.start()
 
     loads[2].wait()
     def norm(i, carry):
@@ -153,30 +160,34 @@
     mine, theirs = pl.ds(0, 256), pl.ds(256, 256)
     go(remote(hn.at[:, mine], hn.at[:, theirs], hx_s, hx_r, at(dc=1)))
 
+    for i in range(2):
+        go(right(i))
+        go(left(i))
+
     local = []
 
-    def select(d):
-        holder = zz(d)
-        name = (y * NZ + holder).astype(jnp.float32)
+    def choose(d):
+        name = (y * NZ + zz(d)).astype(jnp.float32)
         want = lax.broadcasted_iota(jnp.int32, (KEPT, 256), 0).astype(jnp.float32)
-        picks = []
         for k in range(NY):
             hit = info[k, :, 256:512] == name
             v = jnp.max(jnp.where(hit, info[k, :, 0:256], -1.0), axis=0, keepdims=True)
-            picks.append(jnp.where(want == v, 1.0, 0.0).astype(jnp.bfloat16))
-        got = jnp.dot(
-            jnp.concatenate(picks, axis=0),
-            blk[holder].reshape(256, 1024),
-            preferred_element_type=jnp.float32,
-        ).astype(jnp.bfloat16)
+            picks[d % NZ, k * KEPT : (k + 1) * KEPT] = jnp.where(want == v, 1.0, 0.0).astype(
+                jnp.bfloat16
+            )
+
+    def select(d, h):
+        holder, e = zz(d), d % NZ
+        got = jnp.dot(picks[e], blk[holder, h], preferred_element_type=jnp.float32)
+        got = got.astype(jnp.bfloat16)
         for k in range(NY):
-            stage[k, d] = got[k * KEPT : (k + 1) * KEPT]
-        slot = slots_ref.at[y * NZ + holder]
+            stage[k, e, h] = got[k * KEPT : (k + 1) * KEPT]
+        slot = slots_ref.at[y * NZ + holder, h]
         for k in range(1, NY):
-            go(remote(stage.at[k, d], slot, ys_s.at[k, d], ys_r.at[k, d], at(dy=-k)))
-        mine_too = pltpu.make_async_copy(stage.at[0, d], slot, local_sem.at[4 + d])
-        mine_too.start()
-        local.append(mine_too)
+            go(remote(stage.at[k, e, h], slot, ys_s.at[k, e, h], ys_r.at[k, e, h], at(dy=-k)))
+        kept = pltpu.make_async_copy(stage.at[0, e, h], slot, keep_sem.at[e, h])
+        kept.start()
+        local.append(kept)
 
     started = set()
 
@@ -223,14 +234,12 @@
     ones[:, HD:] = jnp.ones((QLEN, HD), jnp.bfloat16)
     token = lax.broadcasted_iota(jnp.int32, (HPB * QLEN, QLEN), 0) % QLEN
     seen = lax.broadcasted_iota(jnp.int32, (HPB * QLEN, QLEN), 1) <= token
-    place = lax.broadcasted_iota(jnp.int32, (QLEN, HD), 1)
 
     def attend_own(n, h):
         query(n, h).wait()
         rows = slice(n * QLEN, (n + 1) * QLEN)
         key = own_ref[rows, h * HD : (h + 1) * HD]
         ones[:, :HD] = own_ref[rows, (KVH + h) * HD : (KVH + h + 1) * HD]
-        packed = jnp.zeros((QLEN, HD), jnp.float32)
         for b in range(GROUPED // HPB):
             cols = [h * WIDTH + (b * HPB + i) * HD for i in range(HPB)]
             q = jnp.concatenate([queries[rows, a : a + HD] for a in cols], axis=0)
@@ -244,61 +253,58 @@
             score = peak + jnp.log2(total) / FACTOR
             for i, a in enumerate(cols):
                 part[rows, a : a + HD] = o[i * QLEN : (i + 1) * QLEN]
-                packed = jnp.where(place == b * HPB + i, score[i * QLEN : (i + 1) * QLEN], packed)
-        lse[n, h] = packed
+                lse[rows, a : a + HD] = score[i * QLEN : (i + 1) * QLEN]
         block = (pl.ds(n * QLEN, QLEN), pl.ds(h * WIDTH, WIDTH))
         for copy in (
             pltpu.make_async_copy(part.at[block], part_ref.at[block], part_sem.at[n, h]),
-            pltpu.make_async_copy(lse.at[n, h], lse_ref.at[n, h], lse_sem.at[n, h]),
+            pltpu.make_async_copy(lse.at[block], lse_ref.at[block], lse_sem.at[n, h]),
         ):
             copy.start()
             local.append(copy)
 
     for k in range(1, NY):
         remote(info.at[k], info.at[k], in_s.at[k], in_r.at[k], at(dy=-k)).wait_recv()
-    own_block.wait()
-    select(0)
+    for d in range(NZ):
+        choose(d)
+    for copy in own_block:
+        copy.wait()
+    select(0, 0)
+    select(0, 1)
+    attend_own(0, 0)
 
     own_w.wait()
     for k in range(1, NZ):
         d = wb.at[x, y, pl.ds(pl.multiple_of(zz(-k) * 128, 128), 128)]
         remote(d, d, wz_s.at[k], wz_r.at[k], at(dz=-k)).wait_recv()
     wx_send(0)
-    for k in range(1, NY):
+    for k in (1, 3):
         go(remote(chunk(0, 0), chunk(0, 0), wy_s.at[k], wy_r.at[k], at(dy=k)))
     remote(hn.at[:, mine], hn.at[:, theirs], hx_s, hx_r, at(dc=1)).wait_recv()
     project(0, 0)
-
-    attend_own(0, 0)
+    attend_own(0, 1)
     z_arrived(0)
     wx_arrived(0)
-    attend_own(0, 1)
     wy_arrived(1)
     wy_arrived(3)
+    go(remote(chunk(0, 0), chunk(0, 0), wy_s.at[2], wy_r.at[2], at(dy=2)))
+    attend_own(0, 2)
     z_arrived(1)
-    select(7)
-    select(1)
+    attend_own(0, 3)
+    wf_arrived(0)
     wy_arrived(2)
-    wf_arrived(0)
-    attend_own(0, 2)
     z_arrived(2)
-    attend_own(0, 3)
+    attend_own(1, 0)
     wx_arrived(1)
+    attend_own(1, 1)
     z_arrived(3)
-    select(6)
-    select(2)
-    attend_own(1, 0)
+    attend_own(1, 2)
     wx_arrived(3)
-    attend_own(1, 1)
+    attend_own(1, 3)
     z_arrived(4)
     wx_arrived(2)
-    attend_own(1, 2)
     wf_arrived(1)
     wf_arrived(3)
-    attend_own(1, 3)
     z_arrived(5)
-    select(5)
-    select(3)
     wf_arrived(2)
 
     for dx in range(NX):
@@ -311,12 +317,13 @@
         local.append(own)
 
     z_arrived(6)
-    select(4)
 
     for k in range(1, NY):
         for d in range(NZ):
-            slot = slots_ref.at[((y + k) % NY) * NZ + zz(d)]
-            remote(stage.at[k, d], slot, ys_s.at[k, d], ys_r.at[k, d], at(dy=k)).wait_recv()
+            for h in range(2):
+                slot = slots_ref.at[((y + k) % NY) * NZ + zz(d), h]
+                src = stage.at[k, d, h]
+                remote(src, slot, ys_s.at[k, d, h], ys_r.at[k, d, h], at(dy=k)).wait_recv()
     for dx in range(NX):
         dst = rec_ref.at[2 * ((x + dx) % NX) + (c + 1) % 2]
         remote(recst.at[dx, theirs], dst, rx_s.at[dx], rx_r.at[dx], at(dc=1)).wait_recv()
@@ -326,57 +333,115 @@
         copy.wait_send()
 
 
-def attend_kernel(ret_ref, q_ref, part_ref, lse_ref, slots_hbm, rec_hbm, out_ref, ctx, vals, sem):
-    n, h = pl.program_id(0), pl.program_id(1)
-    cached = TOPP * KEPT
+def attend_kernel(
+    ret_ref, q_hbm, part_hbm, lse_hbm, slots_hbm, rec_hbm, out_hbm,
+    ctx, vals, queries, part, lse, out, sem, q_sem, part_sem, lse_sem, out_sem,
+):
+    cached, steps = TOPP * KEPT, 2 * KVH
 
     def fetch(i):
         copies = [
             pltpu.make_async_copy(
-                slots_hbm.at[ret_ref[i, j] // 4], ctx.at[i, pl.ds(j * KEPT, KEPT)], sem.at[i, j]
+                slots_hbm.at[ret_ref[i, j] // 4], ctx.at[i, :, pl.ds(j * KEPT, KEPT)], sem.at[i, j]
             )
             for j in range(TOPP)
         ]
         return copies + [
             pltpu.make_async_copy(
                 rec_hbm.at[e, pl.ds(i * QLEN, QLEN)],
-                ctx.at[i, pl.ds(cached, QLEN), pl.ds(e * HD, HD)],
+                ctx.at[i, e // KVH, pl.ds(cached, QLEN), pl.ds(e % KVH * HD, HD)],
                 sem.at[i, TOPP + e],
             )
             for e in range(2 * KVH)
         ]
 
-    for i in range(2):
-
-        @pl.when((n == 0) & (h == 0))
+    def block(t):
+        row = pl.multiple_of(t // KVH * QLEN, QLEN)
+        col = pl.multiple_of(t % KVH * WIDTH, WIDTH)
+        return pl.ds(row, QLEN), pl.ds(col, WIDTH)
+
+    def inputs(t):
+        return [
+            pltpu.make_async_copy(src.at[block(t)], dst.at[block(t)], s.at[t])
+            for src, dst, s in (
+                (q_hbm, queries, q_sem), (part_hbm, part, part_sem), (lse_hbm, lse, lse_sem),
+            )
+        ]
+
+    def output(t):
+        return pltpu.make_async_copy(out.at[block(t)], out_hbm.at[block(t)], out_sem.at[t])
+
+    for copy in fetch(0) + inputs(0) + inputs(1):
+        copy.start()
+    vals[:, HD:] = jnp.ones((TOPP * PLEN, HD), jnp.bfloat16)
+    for copy in fetch(0):
+        copy.wait()
+
+    def step(t, carry):
+        for copy in inputs(t):
+            copy.wait()
+
+        @pl.when(t < steps - 2)
         def _():
-            for copy in fetch(i):
+            for copy in inputs(t + 2):
                 copy.start()
 
-    for i in range(2):
-
-        @pl.when((n == i) & (h == 0))
+        @pl.when(t == 1)
         def _():
-            for copy in fetch(i):
+            for copy in fetch(1):
+                copy.start()
+
+        @pl.when(t == KVH)
+        def _():
+            for copy in fetch(1):
                 copy.wait()
-            vals[:, HD:] = jnp.ones((TOPP * PLEN, HD), jnp.bfloat16)
-
-    key = ctx[n, :, pl.ds(pl.multiple_of(h * HD, HD), HD)]
-    vals[:, :HD] = ctx[n, :, pl.ds(pl.multiple_of((KVH + h) * HD, HD), HD)]
-    for b in range(GROUPED // HPB):
-        heads = [b * HPB + i for i in range(HPB)]
-        q = jnp.concatenate([q_ref[:, i * HD : (i + 1) * HD] for i in heads], axis=0)
-        own = jnp.concatenate([lse_ref[0, 0, :, i : i + 1] for i in heads], axis=0)
-        s = lax.dot_general(q, key, (((1,), (1,)), ((), ())), preferred_element_type=jnp.float32)
-        peak = jnp.maximum(jnp.max(s, axis=1, keepdims=True), own)
-        p = jnp.exp2((s - peak) * FACTOR).astype(jnp.bfloat16)
-        weight = jnp.exp2((own - peak) * FACTOR)
-        o = jnp.dot(p, vals[...], preferred_element_type=jnp.float32)
-        for i, hd in enumerate(heads):
-            rows, cols = slice(i * QLEN, (i + 1) * QLEN), slice(hd * HD, (hd + 1) * HD)
-            w = weight[rows]
-            top = o[rows, :HD] + w * part_ref[:, cols].astype(jnp.float32)
-            out_ref[:, cols] = (top / (o[rows, HD:] + w)).astype(jnp.bfloat16)
+
+        n, h = t // KVH, t % KVH
+        rows = pl.ds(pl.multiple_of(n * QLEN, QLEN), QLEN)
+        head = pl.ds(pl.multiple_of(h * HD, HD), HD)
+        key = ctx[n, 0, :, head]
+        vals[:, :HD] = ctx[n, 1, :, head]
+
+        def cols(b, i):
+            return pl.ds(pl.multiple_of(h * WIDTH + (b * HPA + i) * HD, HD), HD)
+
+        def stack(ref, b):
+            return jnp.concatenate([ref[rows, cols(b, i)] for i in range(HPA)], axis=0)
+
+        def score(b):
+            return lax.dot_general(
+                stack(queries, b), key, (((1,), (1,)), ((), ())), preferred_element_type=jnp.float32
+            )
+
+        def finish(b, s):
+            own = stack(lse, b)
+            peak = jnp.maximum(jnp.max(s, axis=1, keepdims=True), own)
+            p = jnp.concatenate(
+                [
+                    jnp.exp2((s[:, c : c + HD] - peak) * FACTOR).astype(jnp.bfloat16)
+                    for c in range(0, TOPP * PLEN, HD)
+                ],
+                axis=1,
+            )
+            weight = jnp.exp2((own - peak) * FACTOR)
+            o = jnp.dot(p, vals[...], preferred_element_type=jnp.float32)
+            top = o[:, :HD] + weight * stack(part, b).astype(jnp.float32)
+            o = (top / (o[:, HD:] + weight)).astype(jnp.bfloat16)
+            for i in range(HPA):
+                out[rows, cols(b, i)] = o[i * QLEN : (i + 1) * QLEN]
+
+        groups = GROUPED // HPA
+        s = score(0)
+        for b in range(groups):
+            later = score(b + 1) if b + 1 < groups else None
+            finish(b, s)
+            s = later
+        output(t).start()
+        return carry
+
+    lax.fori_loop(0, steps, step, 0)
+    for t in range(steps):
+        output(t).wait()
 
 
 def communicate(retrieval, cache, hidden, w_kv, positions, q, own):
@@ -385,33 +450,34 @@
     return pl.pallas_call(
         comm_kernel,
         out_shape=(
-            jax.ShapeDtypeStruct((NY * NZ, KEPT, 1024), bf),
+            jax.ShapeDtypeStruct((NY * NZ, 2, KEPT, HALF), bf),
             jax.ShapeDtypeStruct((8, 256, 128), bf),
             jax.ShapeDtypeStruct(q.shape, bf),
-            jax.ShapeDtypeStruct((2, KVH, QLEN, HD), f32),
+            jax.ShapeDtypeStruct(q.shape, f32),
         ),
         in_specs=[pl.BlockSpec(memory_space=pltpu.SMEM)] + [hbm] * 6,
         out_specs=(hbm,) * 4,
         scratch_shapes=[
-            pltpu.VMEM((NZ, 2, 128, 1024), bf),
+            pltpu.VMEM((NZ, 2, 256, HALF), bf),
             pltpu.VMEM((NX, NY, 1024, 128), bf),
             pltpu.VMEM((4, 512, 1024), bf),
             pltpu.VMEM((NX, 512, 128), f32),
-            pltpu.VMEM((NY, NZ, KEPT, 1024), bf),
+            pltpu.VMEM((NY, NZ, 2, KEPT, HALF), bf),
             pltpu.VMEM((NX, 512, 128), bf),
             pltpu.VMEM((NY, 16, 512), f32),
+            pltpu.VMEM((NZ, NY * KEPT, 256), bf),
             pltpu.VMEM(hidden.shape, bf),
             pltpu.VMEM(positions.shape, jnp.int32),
             pltpu.VMEM(q.shape, bf),
             pltpu.VMEM(own.shape, bf),
             pltpu.VMEM((QLEN, 2 * HD), bf),
             pltpu.VMEM(q.shape, bf),
-            pltpu.VMEM((2, KVH, QLEN, HD), f32),
-            dma((16,)), dma((3,)), dma((2, KVH)), dma((2, KVH)), dma((2, KVH)),
+            pltpu.VMEM(q.shape, f32),
+            dma((16,)), dma((3,)), dma((2, KVH)), dma((2, KVH)), dma((2, KVH)), dma((NZ, 2)),
             dma((NZ,)), dma((NZ,)), dma((NY,)), dma((NY,)),
             dma((2, NY)), dma((2, NY)), dma((NY,)), dma((NY,)),
             dma((NY,)), dma((NY,)), dma((7,)), dma((7,)), dma((7,)), dma((7,)),
-            dma((NY, NZ)), dma((NY, NZ)), dma, dma, dma((NX,)), dma((NX,)),
+            dma((NY, NZ, 2)), dma((NY, NZ, 2)), dma, dma, dma((NX,)), dma((NX,)),
         ],
         compiler_params=pltpu.CompilerParams(
             collective_id=0, has_side_effects=True, vmem_limit_bytes=56 << 20
@@ -421,28 +487,22 @@
 
 
 def attend(retrieval, q, part, lse, slots, rec):
+    dma, bf = pltpu.SemaphoreType.DMA, jnp.bfloat16
     hbm = pl.BlockSpec(memory_space=pltpu.HBM)
-    wide = pl.BlockSpec((QLEN, WIDTH), lambda n, h, s: (n, h))
     return pl.pallas_call(
         attend_kernel,
         out_shape=jax.ShapeDtypeStruct(q.shape, q.dtype),
-        grid_spec=pltpu.PrefetchScalarGridSpec(
-            num_scalar_prefetch=1,
-            grid=(2, KVH),
-            in_specs=[
-                wide,
-                wide,
-                pl.BlockSpec((1, 1, QLEN, HD), lambda n, h, s: (n, h, 0, 0)),
-                hbm,
-                hbm,
-            ],
-            out_specs=wide,
-            scratch_shapes=[
-                pltpu.VMEM((2, TOPP * PLEN, 1024), jnp.bfloat16),
-                pltpu.VMEM((TOPP * PLEN, 2 * HD), jnp.bfloat16),
-                pltpu.SemaphoreType.DMA((2, 16)),
-            ],
-        ),
+        in_specs=[pl.BlockSpec(memory_space=pltpu.SMEM)] + [hbm] * 5,
+        out_specs=hbm,
+        scratch_shapes=[
+            pltpu.VMEM((2, 2, TOPP * PLEN, HALF), bf),
+            pltpu.VMEM((TOPP * PLEN, 2 * HD), bf),
+            pltpu.VMEM(q.shape, bf),
+            pltpu.VMEM(q.shape, bf),
+            pltpu.VMEM(q.shape, jnp.float32),
+            pltpu.VMEM(q.shape, bf),
+            dma((2, TOPP + 2 * KVH)), dma((8,)), dma((8,)), dma((8,)), dma((8,)),
+        ],
         compiler_params=pltpu.CompilerParams(vmem_limit_bytes=56 << 20),
         name="attend",
     )(retrieval, q, part, lse, slots, rec)
@@ -451,7 +511,7 @@
 def local(q_rows, own_kv, cache, recomp_hidden, w_kv, retrieval, positions):
     slots, rec, part, lse = communicate(
         retrieval,
-        cache.reshape(2, 128, 1024),
+        cache.reshape(256, 1024),
         recomp_hidden.reshape(256, D),
         w_kv,
         positions,

time: 102 us -> 85.2 us (0.84)
  Pallas kernels: 102 us -> 85 us
    pallas_call x1, Pallas kernels: 30.8 us -> 18.2 us  [attend(): pl.pallas_call(attend_kernel, out_shape=jax.ShapeDtypeStruct(q.shape, q.d...]
    pallas_call x1, Pallas kernels: 71.1 us -> 66.8 us  [communicate(): pl.pallas_call(comm_kernel, out_shape=(jax.ShapeDtypeStruct((NY * NZ, 2,...]
where the time goes in v3:
time: 85.2 us; the launch traced here: 85.1 us
  Pallas kernels  85 us (100%)
    pallas_call x1, Pallas kernels, communicate(): pl.pallas_call(comm_kernel, out_shape=(jax.ShapeDtypeStruct((NY * NZ, 2,...  66.8 us
    pallas_call x1, Pallas kernels, attend(): pl.pallas_call(attend_kernel, out_shape=jax.ShapeDtypeStruct(q.shape, q.d...  18.2 us

profile of v3, /device:TPU:8, one launch (start us, length us, event | category | flops | bytes accessed | tf_op | source)
XLA Modules:
  0.0 85.1 jit_solution(4168007257561992823)
XLA Ops:
  0.0 66.8 %exchange.1 = (bf16[32,2,48,512]{3,2,1,0:T(8,128)(2,1)}, bf16[8,256,128]{2,1,0:T(8,128)(2,1)}, bf16[256,8192]{1,0:T(8,128)(2,1)}, f32[256,8192]{1,0:T(8,128)}) custom-call(s32[2,8]{1,0:T(2,128)} %ret_ref.3, bf16[256,1024]{1,0:T(8,128)(2,1)} %bitcast.3, bf16[256,4096]{1,0:T(8,128)(2,1)} %bitcast.2, bf16[128,128]{1,0:T(8,128)(2,1)} %w_ref.1, ...), custom_call_target="tpu_custom_call" | custom-call | tf_op jit(solution)/shard_map/exchange/pallas_call | solution.py:450
  66.8 18.2 %attend.1 = bf16[256,8192]{1,0:T(8,128)(2,1)} custom-call(s32[2,8]{1,0:T(2,128)} %ret_ref.3, bf16[256,8192]{1,0:T(8,128)(2,1)} %q_hbm.3, bf16[256,8192]{1,0:T(8,128)(2,1)} %get-tuple-element.9.part_hbm, f32[256,8192]{1,0:T(8,128)} %get-tuple-element.10.lse_hbm, bf16[32,2,48,512]{3,2,1,0:T(8,128)(2,1)} %get-tuple-element.11.slots_hbm, ...), custom_call_target="tpu_custom_call" | custom-call | tf_op jit(solution)/shard_map/attend/pallas_call | solution.py:492

commit v4 on v3

--- a/solution.py
+++ b/solution.py
@@ -22,7 +22,8 @@
 NX, NY, NZ = 4, 4, 8
 HPB = 8
 HPA = 4
-HALF = KVH * HD
+PARTS = 4
+PART = 2 * KVH * HD // PARTS
 GROUPED = HQ // KVH
 WIDTH = GROUPED * HD
 FACTOR = LOG2E / HD**0.5
@@ -63,7 +64,7 @@
         block = (pl.ds(n * QLEN, QLEN), pl.ds(h * WIDTH, WIDTH))
         return pltpu.make_async_copy(q_hbm.at[block], queries.at[block], q_sem.at[n, h])
 
-    peers = [at(dz=k) for k in range(1, NZ)] + [at(dy=k) for k in range(1, NY)]
+    peers = [at(dz=k) for k in (1, 2, -2, -1)] + [at(dy=k) for k in range(1, NY)]
     peers += [at(dx=1), at(dx=-1), at(dc=1)]
     barrier = pltpu.get_barrier_semaphore()
     for dev in peers:
@@ -99,49 +100,53 @@
     pl.semaphore_wait(barrier, len(peers))
 
     zrow = pl.multiple_of(z * 128, 128)
-    for k in range(1, NZ):
-        go(remote(w_ref, wb.at[x, y, pl.ds(zrow, 128)], wz_s.at[k], wz_r.at[k], at(dz=k)))
+    for k in (1, 2, 6, 7):
+        dst = wb.at[x, y, pl.ds(zrow, 128)]
+        go(remote(w_ref, dst, wz_s.at[k], wz_r.at[k], at(dz=k if k < 4 else k - NZ)))
     for k in range(1, NY):
         go(remote(info.at[0], info.at[k], in_s.at[k], in_r.at[k], at(dy=k)))
 
-    def half_right(i):
-        return 0 if i == 6 else i % 2
-
-    def half_left(i):
-        return 1 if i == 6 else 1 - i % 2
+    last = 3 * PARTS
+
+    def part_right(i):
+        return i % PARTS
+
+    def part_left(i):
+        return PARTS - 1 - i % PARTS
 
     def zz(d):
         return (z + d + NZ) % NZ
 
-    def own_half(h):
-        return cache_ref.at[:, pl.ds(h * HALF, HALF)]
+    def own_part(h):
+        return cache_ref.at[:, pl.ds(h * PART, PART)]
 
     def right(i):
-        h = half_right(i)
-        dst = blk.at[zz(-(i // 2)), h]
-        return remote(own_half(h) if i < 2 else dst, dst, zr_s.at[i], zr_r.at[i], at(dz=1))
+        h = part_right(i)
+        dst = blk.at[zz(-(i // PARTS)), h]
+        return remote(own_part(h) if i < PARTS else dst, dst, zr_s.at[i], zr_r.at[i], at(dz=1))
 
     def left(i):
-        h = half_left(i)
-        dst = blk.at[zz(i // 2), h]
-        return remote(own_half(h) if i < 2 else dst, dst, zl_s.at[i], zl_r.at[i], at(dz=-1))
+        h = part_left(i)
+        dst = blk.at[zz(i // PARTS), h]
+        return remote(own_part(h) if i < PARTS else dst, dst, zl_s.at[i], zl_r.at[i], at(dz=-1))
 
     def z_arrived(i):
-        d = blk.at[zz(-1 - i // 2), half_right(i)]
+        d = blk.at[zz(-1 - i // PARTS), part_right(i)]
         remote(d, d, zr_s.at[i], zr_r.at[i], at(dz=-1)).wait_recv()
-        if i + 2 <= 6:
-            go(right(i + 2))
-        d = blk.at[zz(1 + i // 2), half_left(i)]
+        if i + PARTS < last + PARTS // 2:
+            go(right(i + PARTS))
+        d = blk.at[zz(1 + i // PARTS), part_left(i)]
         remote(d, d, zl_s.at[i], zl_r.at[i], at(dz=1)).wait_recv()
-        if i + 2 <= 6:
-            go(left(i + 2))
-        select(-1 - i // 2, half_right(i))
-        select(1 + i // 2, half_left(i))
+        if i + PARTS < last + PARTS // 2:
+            go(left(i + PARTS))
+        select(-1 - i // PARTS, part_right(i))
+        select(1 + i // PARTS, part_left(i))
 
     own_w = pltpu.make_async_copy(w_ref, wb.at[x, y, pl.ds(zrow, 128)], local_sem.at[1])
     own_w.start()
     own_block = [
-        pltpu.make_async_copy(own_half(h), blk.at[z, h], local_sem.at[2 + h]) for h in range(2)
+        pltpu.make_async_copy(own_part(h), blk.at[z, h], local_sem.at[2 + h])
+        for h in range(PARTS)
     ]
     for copy in own_block:
         copy.start()
@@ -160,9 +165,26 @@
     mine, theirs = pl.ds(0, 256), pl.ds(256, 256)
     go(remote(hn.at[:, mine], hn.at[:, theirs], hx_s, hx_r, at(dc=1)))
 
-    for i in range(2):
+    for i in range(PARTS):
         go(right(i))
         go(left(i))
+
+    def w_row(k):
+        return wb.at[x, y, pl.ds(pl.multiple_of(zz(-k) * 128, 128), 128)]
+
+    def wz_arrived(k):
+        d = w_row(k)
+        remote(d, d, wz_s.at[k], wz_r.at[k], at(dz=-k if k < 4 else NZ - k)).wait_recv()
+
+    def wz_forward(k, steps):
+        j = (k + steps) % NZ
+        go(remote(w_row(k), w_row(k), wz_s.at[j], wz_r.at[j], at(dz=steps)))
+
+    wz_arrived(2)
+    wz_forward(2, 1)
+    wz_forward(2, 2)
+    wz_arrived(6)
+    wz_forward(6, -1)
 
     local = []
 
@@ -184,10 +206,8 @@
             stage[k, e, h] = got[k * KEPT : (k + 1) * KEPT]
         slot = slots_ref.at[y * NZ + holder, h]
         for k in range(1, NY):
-            go(remote(stage.at[k, e, h], slot, ys_s.at[k, e, h], ys_r.at[k, e, h], at(dy=-k)))
-        kept = pltpu.make_async_copy(stage.at[0, e, h], slot, keep_sem.at[e, h])
-        kept.start()
-        local.append(kept)
+            remote(stage.at[k, e, h], slot, ys_s.at[k], ys_r.at[k], at(dy=-k)).start()
+        pltpu.make_async_copy(stage.at[0, e, h], slot, keep_sem).start()
 
     started = set()
 
@@ -268,43 +288,49 @@
         choose(d)
     for copy in own_block:
         copy.wait()
-    select(0, 0)
-    select(0, 1)
+    for h in range(PARTS):
+        select(0, h)
     attend_own(0, 0)
 
     own_w.wait()
-    for k in range(1, NZ):
-        d = wb.at[x, y, pl.ds(pl.multiple_of(zz(-k) * 128, 128), 128)]
-        remote(d, d, wz_s.at[k], wz_r.at[k], at(dz=-k)).wait_recv()
+    for k in (1, 7, 3, 5, 4):
+        wz_arrived(k)
     wx_send(0)
     for k in (1, 3):
         go(remote(chunk(0, 0), chunk(0, 0), wy_s.at[k], wy_r.at[k], at(dy=k)))
     remote(hn.at[:, mine], hn.at[:, theirs], hx_s, hx_r, at(dc=1)).wait_recv()
     project(0, 0)
+    z_arrived(0)
+    z_arrived(1)
     attend_own(0, 1)
-    z_arrived(0)
     wx_arrived(0)
     wy_arrived(1)
     wy_arrived(3)
     go(remote(chunk(0, 0), chunk(0, 0), wy_s.at[2], wy_r.at[2], at(dy=2)))
+    z_arrived(2)
+    z_arrived(3)
     attend_own(0, 2)
-    z_arrived(1)
+    z_arrived(4)
+    wf_arrived(0)
     attend_own(0, 3)
-    wf_arrived(0)
+    z_arrived(5)
     wy_arrived(2)
-    z_arrived(2)
+    z_arrived(6)
     attend_own(1, 0)
     wx_arrived(1)
+    z_arrived(7)
     attend_own(1, 1)
-    z_arrived(3)
+    z_arrived(8)
+    wx_arrived(3)
     attend_own(1, 2)
-    wx_arrived(3)
+    z_arrived(9)
     attend_own(1, 3)
-    z_arrived(4)
+    z_arrived(10)
     wx_arrived(2)
+    z_arrived(11)
     wf_arrived(1)
     wf_arrived(3)
-    z_arrived(5)
+    z_arrived(12)
     wf_arrived(2)
 
     for dx in range(NX):
@@ -316,14 +342,8 @@
         own.start()
         local.append(own)
 
-    z_arrived(6)
-
-    for k in range(1, NY):
-        for d in range(NZ):
-            for h in range(2):
-                slot = slots_ref.at[((y + k) % NY) * NZ + zz(d), h]
-                src = stage.at[k, d, h]
-                remote(src, slot, ys_s.at[k, d, h], ys_r.at[k, d, h], at(dy=k)).wait_recv()
+    z_arrived(13)
+
     for dx in range(NX):
         dst = rec_ref.at[2 * ((x + dx) % NX) + (c + 1) % 2]
         remote(recst.at[dx, theirs], dst, rx_s.at[dx], rx_r.at[dx], at(dc=1)).wait_recv()
@@ -331,6 +351,11 @@
         copy.wait()
     for copy in sends:
         copy.wait_send()
+    pltpu.make_async_copy(stage.at[0], slots_ref.at[pl.ds(y * NZ, NZ)], keep_sem).wait()
+    for k in range(1, NY):
+        rows = slots_ref.at[pl.ds((y + k) % NY * NZ, NZ)]
+        remote(stage.at[k], rows, ys_s.at[k], ys_r.at[k], at(dy=-k)).wait_send()
+        remote(stage.at[k], rows, ys_s.at[k], ys_r.at[k], at(dy=k)).wait_recv()
 
 
 def attend_kernel(
@@ -349,7 +374,7 @@
         return copies + [
             pltpu.make_async_copy(
                 rec_hbm.at[e, pl.ds(i * QLEN, QLEN)],
-                ctx.at[i, e // KVH, pl.ds(cached, QLEN), pl.ds(e % KVH * HD, HD)],
+                ctx.at[i, e // 2, pl.ds(cached, QLEN), pl.ds(e % 2 * HD, HD)],
                 sem.at[i, TOPP + e],
             )
             for e in range(2 * KVH)
@@ -371,11 +396,13 @@
     def output(t):
         return pltpu.make_async_copy(out.at[block(t)], out_hbm.at[block(t)], out_sem.at[t])
 
-    for copy in fetch(0) + inputs(0) + inputs(1):
+    for copy in fetch(0) + inputs(0):
         copy.start()
     vals[:, HD:] = jnp.ones((TOPP * PLEN, HD), jnp.bfloat16)
     for copy in fetch(0):
         copy.wait()
+    for copy in inputs(1):
+        copy.start()
 
     def step(t, carry):
         for copy in inputs(t):
@@ -398,9 +425,9 @@
 
         n, h = t // KVH, t % KVH
         rows = pl.ds(pl.multiple_of(n * QLEN, QLEN), QLEN)
-        head = pl.ds(pl.multiple_of(h * HD, HD), HD)
-        key = ctx[n, 0, :, head]
-        vals[:, :HD] = ctx[n, 1, :, head]
+        head = pl.ds(pl.multiple_of(h % 2 * HD, HD), HD)
+        key = ctx[n, h // 2, :, head]
+        vals[:, :HD] = ctx[n, 2 + h // 2, :, head]
 
         def cols(b, i):
             return pl.ds(pl.multiple_of(h * WIDTH + (b * HPA + i) * HD, HD), HD)
@@ -450,7 +477,7 @@
     return pl.pallas_call(
         comm_kernel,
         out_shape=(
-            jax.ShapeDtypeStruct((NY * NZ, 2, KEPT, HALF), bf),
+            jax.ShapeDtypeStruct((NY * NZ, PARTS, KEPT, PART), bf),
             jax.ShapeDtypeStruct((8, 256, 128), bf),
             jax.ShapeDtypeStruct(q.shape, bf),
             jax.ShapeDtypeStruct(q.shape, f32),
@@ -458,11 +485,11 @@
         in_specs=[pl.BlockSpec(memory_space=pltpu.SMEM)] + [hbm] * 6,
         out_specs=(hbm,) * 4,
         scratch_shapes=[
-            pltpu.VMEM((NZ, 2, 256, HALF), bf),
+            pltpu.VMEM((NZ, PARTS, 256, PART), bf),
             pltpu.VMEM((NX, NY, 1024, 128), bf),
             pltpu.VMEM((4, 512, 1024), bf),
             pltpu.VMEM((NX, 512, 128), f32),
-            pltpu.VMEM((NY, NZ, 2, KEPT, HALF), bf),
+            pltpu.VMEM((NY, NZ, PARTS, KEPT, PART), bf),
             pltpu.VMEM((NX, 512, 128), bf),
             pltpu.VMEM((NY, 16, 512), f32),
             pltpu.VMEM((NZ, NY * KEPT, 256), bf),
@@ -473,11 +500,11 @@
             pltpu.VMEM((QLEN, 2 * HD), bf),
             pltpu.VMEM(q.shape, bf),
             pltpu.VMEM(q.shape, f32),
-            dma((16,)), dma((3,)), dma((2, KVH)), dma((2, KVH)), dma((2, KVH)), dma((NZ, 2)),
+            dma((16,)), dma((3,)), dma((2, KVH)), dma((2, KVH)), dma((2, KVH)), dma,
             dma((NZ,)), dma((NZ,)), dma((NY,)), dma((NY,)),
             dma((2, NY)), dma((2, NY)), dma((NY,)), dma((NY,)),
-            dma((NY,)), dma((NY,)), dma((7,)), dma((7,)), dma((7,)), dma((7,)),
-            dma((NY, NZ, 2)), dma((NY, NZ, 2)), dma, dma, dma((NX,)), dma((NX,)),
+            dma((NY,)), dma((NY,)), dma((14,)), dma((14,)), dma((14,)), dma((14,)),
+            dma((NY,)), dma((NY,)), dma, dma, dma((NX,)), dma((NX,)),
         ],
         compiler_params=pltpu.CompilerParams(
             collective_id=0, has_side_effects=True, vmem_limit_bytes=56 << 20
@@ -495,7 +522,7 @@
         in_specs=[pl.BlockSpec(memory_space=pltpu.SMEM)] + [hbm] * 5,
         out_specs=hbm,
         scratch_shapes=[
-            pltpu.VMEM((2, 2, TOPP * PLEN, HALF), bf),
+            pltpu.VMEM((2, PARTS, TOPP * PLEN, PART), bf),
             pltpu.VMEM((TOPP * PLEN, 2 * HD), bf),
             pltpu.VMEM(q.shape, bf),
             pltpu.VMEM(q.shape, bf),

time: 85.2 us -> 90.2 us (1.059)
  Pallas kernels: 85 us -> 89.5 us
    pallas_call x1, Pallas kernels: 66.8 us -> 71.3 us  [communicate(): pl.pallas_call(comm_kernel, out_shape=(jax.ShapeDtypeStruct((NY * NZ, PAR...]
where the time goes in v4:
time: 90.2 us; the launch traced here: 89.7 us
  Pallas kernels  89.5 us (99%)
    pallas_call x1, Pallas kernels, communicate(): pl.pallas_call(comm_kernel, out_shape=(jax.ShapeDtypeStruct((NY * NZ, PAR...  71.3 us
    pallas_call x1, Pallas kernels, attend(): pl.pallas_call(attend_kernel, out_shape=jax.ShapeDtypeStruct(q.shape, q.d...  18.2 us

profile of v4, /device:TPU:8, one launch (start us, length us, event | category | flops | bytes accessed | tf_op | source)
XLA Modules:
  0.0 89.7 jit_solution(5530365255310212936)
XLA Ops:
  0.0 71.3 %exchange.1 = (bf16[32,4,48,256]{3,2,1,0:T(8,128)(2,1)}, bf16[8,256,128]{2,1,0:T(8,128)(2,1)}, bf16[256,8192]{1,0:T(8,128)(2,1)}, f32[256,8192]{1,0:T(8,128)}) custom-call(s32[2,8]{1,0:T(2,128)} %ret_ref.3, bf16[256,1024]{1,0:T(8,128)(2,1)} %bitcast.3, bf16[256,4096]{1,0:T(8,128)(2,1)} %bitcast.2, bf16[128,128]{1,0:T(8,128)(2,1)} %w_ref.1, ...), custom_call_target="tpu_custom_call" | custom-call | tf_op jit(solution)/shard_map/exchange/pallas_call | solution.py:477
  71.3 18.2 %attend.1 = bf16[256,8192]{1,0:T(8,128)(2,1)} custom-call(s32[2,8]{1,0:T(2,128)} %ret_ref.3, bf16[256,8192]{1,0:T(8,128)(2,1)} %q_hbm.3, bf16[256,8192]{1,0:T(8,128)(2,1)} %get-tuple-element.9.part_hbm, f32[256,8192]{1,0:T(8,128)} %get-tuple-element.10.lse_hbm, bf16[32,4,48,256]{3,2,1,0:T(8,128)(2,1)} %get-tuple-element.11.slots_hbm, ...), custom_call_target="tpu_custom_call" | custom-call | tf_op jit(solution)/shard_map/attend/pallas_call | solution.py:519

commit v5 on v4

--- a/solution.py
+++ b/solution.py
@@ -64,7 +64,7 @@
         block = (pl.ds(n * QLEN, QLEN), pl.ds(h * WIDTH, WIDTH))
         return pltpu.make_async_copy(q_hbm.at[block], queries.at[block], q_sem.at[n, h])
 
-    peers = [at(dz=k) for k in (1, 2, -2, -1)] + [at(dy=k) for k in range(1, NY)]
+    peers = [at(dz=k) for k in range(1, NZ)] + [at(dy=k) for k in range(1, NY)]
     peers += [at(dx=1), at(dx=-1), at(dc=1)]
     barrier = pltpu.get_barrier_semaphore()
     for dev in peers:
@@ -100,9 +100,9 @@
     pl.semaphore_wait(barrier, len(peers))
 
     zrow = pl.multiple_of(z * 128, 128)
-    for k in (1, 2, 6, 7):
+    for k in range(1, NZ):
         dst = wb.at[x, y, pl.ds(zrow, 128)]
-        go(remote(w_ref, dst, wz_s.at[k], wz_r.at[k], at(dz=k if k < 4 else k - NZ)))
+        go(remote(w_ref, dst, wz_s.at[k], wz_r.at[k], at(dz=k)))
     for k in range(1, NY):
         go(remote(info.at[0], info.at[k], in_s.at[k], in_r.at[k], at(dy=k)))
 
@@ -180,11 +180,6 @@
         j = (k + steps) % NZ
         go(remote(w_row(k), w_row(k), wz_s.at[j], wz_r.at[j], at(dz=steps)))
 
-    wz_arrived(2)
-    wz_forward(2, 1)
-    wz_forward(2, 2)
-    wz_arrived(6)
-    wz_forward(6, -1)
 
     local = []
 
@@ -293,7 +288,7 @@
     attend_own(0, 0)
 
     own_w.wait()
-    for k in (1, 7, 3, 5, 4):
+    for k in range(1, NZ):
         wz_arrived(k)
     wx_send(0)
     for k in (1, 3):

time: 90.2 us -> 81.4 us (0.902)
  Pallas kernels: 89.5 us -> 80.9 us
    pallas_call x1, Pallas kernels: 71.3 us -> 62.7 us  [communicate(): pl.pallas_call(comm_kernel, out_shape=(jax.ShapeDtypeStruct((NY * NZ, PAR...]
where the time goes in v5:
time: 81.4 us; the launch traced here: 81 us
  Pallas kernels  80.9 us (99%)
    pallas_call x1, Pallas kernels, communicate(): pl.pallas_call(comm_kernel, out_shape=(jax.ShapeDtypeStruct((NY * NZ, PAR...  62.7 us
    pallas_call x1, Pallas kernels, attend(): pl.pallas_call(attend_kernel, out_shape=jax.ShapeDtypeStruct(q.shape, q.d...  18.1 us

profile of v5, /device:TPU:8, one launch (start us, length us, event | category | flops | bytes accessed | tf_op | source)
XLA Modules:
  0.0 81.0 jit_solution(320471564121985555)
XLA Ops:
  0.0 62.7 %exchange.1 = (bf16[32,4,48,256]{3,2,1,0:T(8,128)(2,1)}, bf16[8,256,128]{2,1,0:T(8,128)(2,1)}, bf16[256,8192]{1,0:T(8,128)(2,1)}, f32[256,8192]{1,0:T(8,128)}) custom-call(s32[2,8]{1,0:T(2,128)} %ret_ref.3, bf16[256,1024]{1,0:T(8,128)(2,1)} %bitcast.3, bf16[256,4096]{1,0:T(8,128)(2,1)} %bitcast.2, bf16[128,128]{1,0:T(8,128)(2,1)} %w_ref.1, ...), custom_call_target="tpu_custom_call" | custom-call | tf_op jit(solution)/shard_map/exchange/pallas_call | solution.py:472
  62.7 18.1 %attend.1 = bf16[256,8192]{1,0:T(8,128)(2,1)} custom-call(s32[2,8]{1,0:T(2,128)} %ret_ref.3, bf16[256,8192]{1,0:T(8,128)(2,1)} %q_hbm.3, bf16[256,8192]{1,0:T(8,128)(2,1)} %get-tuple-element.9.part_hbm, f32[256,8192]{1,0:T(8,128)} %get-tuple-element.10.lse_hbm, bf16[32,4,48,256]{3,2,1,0:T(8,128)(2,1)} %get-tuple-element.11.slots_hbm, ...), custom_call_target="tpu_custom_call" | custom-call | tf_op jit(solution)/shard_map/attend/pallas_call | solution.py:514

commit v6 on v5

--- a/solution.py
+++ b/solution.py
@@ -277,6 +277,12 @@
             copy.start()
             local.append(copy)
 
+    own_w.wait()
+    for k in range(1, NZ):
+        wz_arrived(k)
+    wx_send(0)
+    for k in (1, 3):
+        go(remote(chunk(0, 0), chunk(0, 0), wy_s.at[k], wy_r.at[k], at(dy=k)))
     for k in range(1, NY):
         remote(info.at[k], info.at[k], in_s.at[k], in_r.at[k], at(dy=-k)).wait_recv()
     for d in range(NZ):
@@ -287,12 +293,6 @@
         select(0, h)
     attend_own(0, 0)
 
-    own_w.wait()
-    for k in range(1, NZ):
-        wz_arrived(k)
-    wx_send(0)
-    for k in (1, 3):
-        go(remote(chunk(0, 0), chunk(0, 0), wy_s.at[k], wy_r.at[k], at(dy=k)))
     remote(hn.at[:, mine], hn.at[:, theirs], hx_s, hx_r, at(dc=1)).wait_recv()
     project(0, 0)
     z_arrived(0)

time: 81.4 us -> 83.3 us (1.023)
  Pallas kernels: 80.9 us -> 82.1 us
    pallas_call x1, Pallas kernels: 62.7 us -> 63.9 us  [communicate(): pl.pallas_call(comm_kernel, out_shape=(jax.ShapeDtypeStruct((NY * NZ, PAR...]
where the time goes in v6:
time: 83.3 us; the launch traced here: 82.2 us
  Pallas kernels  82.1 us (99%)
    pallas_call x1, Pallas kernels, communicate(): pl.pallas_call(comm_kernel, out_shape=(jax.ShapeDtypeStruct((NY * NZ, PAR...  63.9 us
    pallas_call x1, Pallas kernels, attend(): pl.pallas_call(attend_kernel, out_shape=jax.ShapeDtypeStruct(q.shape, q.d...  18.1 us

profile of v6, /device:TPU:8, one launch (start us, length us, event | category | flops | bytes accessed | tf_op | source)
XLA Modules:
  0.0 82.2 jit_solution(8574402113275564701)
XLA Ops:
  0.0 63.9 %exchange.1 = (bf16[32,4,48,256]{3,2,1,0:T(8,128)(2,1)}, bf16[8,256,128]{2,1,0:T(8,128)(2,1)}, bf16[256,8192]{1,0:T(8,128)(2,1)}, f32[256,8192]{1,0:T(8,128)}) custom-call(s32[2,8]{1,0:T(2,128)} %ret_ref.3, bf16[256,1024]{1,0:T(8,128)(2,1)} %bitcast.3, bf16[256,4096]{1,0:T(8,128)(2,1)} %bitcast.2, bf16[128,128]{1,0:T(8,128)(2,1)} %w_ref.1, ...), custom_call_target="tpu_custom_call" | custom-call | tf_op jit(solution)/shard_map/exchange/pallas_call | solution.py:472
  63.9 18.1 %attend.1 = bf16[256,8192]{1,0:T(8,128)(2,1)} custom-call(s32[2,8]{1,0:T(2,128)} %ret_ref.3, bf16[256,8192]{1,0:T(8,128)(2,1)} %q_hbm.3, bf16[256,8192]{1,0:T(8,128)(2,1)} %get-tuple-element.9.part_hbm, f32[256,8192]{1,0:T(8,128)} %get-tuple-element.10.lse_hbm, bf16[32,4,48,256]{3,2,1,0:T(8,128)(2,1)} %get-tuple-element.11.slots_hbm, ...), custom_call_target="tpu_custom_call" | custom-call | tf_op jit(solution)/shard_map/attend/pallas_call | solution.py:514
